TPU v7x, 256 devices: a whole 4x4x8 slice. The times are simulated.
256 devices in a mesh: loop: 32 (over z, x_lo, core), own: 8 (over x_hi, y).
Axes of the slice: x: 4 (x_hi: 2, x_lo: 2; x = x_hi * 2 + x_lo), y: 4, z: 8, core: 2. Of those that a mesh axis runs over, the one named last changes fastest.
Arguments:
- factor_start: float32 [8192, 128], P(('loop', 'own')), may hold values from -6 to 6
- activity: float32 [8192], P(('loop', 'own')), may hold values from 0.05 to 2
- word_factors: bfloat16 [32, 8, 128, 128], P('loop'), may hold values from -0.03125 to 0.03125
- sub_factors: bfloat16 [2048, 128], replicated, may hold values from -6 to 6
- ratings: bfloat16 [32, 8, 32, 8, 128, 128], P('loop', 'own'), may hold values from -6 to 6
- user_tile: int32 [32, 8, 32, 8], P('loop', 'own'), may hold values from 0 to 1
- word_tile: int32 [32, 8, 32, 8], P('loop', 'own'), may hold values from 0 to 7
- subreddit: int32 [32, 8, 32, 8], P('loop', 'own'), may hold values from 0 to 2047
- counts: int32 [32, 8, 32], P('loop', 'own'), may hold values from 1 to 8
- runs: int32 [32, 8, 32, 8, 2, 128], P('loop', 'own'), may hold values from 0 to 128, as said below
Outputs:
- solution: float32 [8192, 128], P(('loop', 'own'))
- residual: float32 [8192, 128], P(('loop', 'own'))
Inputs may be any that keep to these rules, and one draw needn't show every extreme that they name: runs[..., 0, a] is the first observed column of row a of a block and runs[..., 1, a] the number of observed columns, counted cyclically from it; each block has a row observed in full.
All inputs are finite; a program needn't handle non-finite values.
Results may differ from a plain program's by a relative error of at most 0.03.
Values may be sent and summed in bfloat16 or wider, within the bound.
A program may use at most 128 MiB of HBM per device.

v0:
```python
import jax
import jax.numpy as jnp
from jax import lax
from jax.sharding import PartitionSpec as P

TILE = 128
UT = 2
SLOTS = 8
ITERS = 2


ridge = 0.05


def on_device(
    factor_start,
    activity,
    word_factors,
    sub_factors,
    ratings,
    user_tile,
    word_tile,
    subreddit,
    counts,
    runs,
):
    group_rows = UT * TILE
    groups = lax.axis_size("loop")
    word_rows = word_factors[0][word_tile[0, 0]]
    sub_rows = sub_factors[subreddit[0, 0]]
    products = (word_rows.astype(jnp.float32) * sub_rows[:, :, None, :].astype(jnp.float32)).astype(
        jnp.bfloat16
    )
    slot_live = jnp.arange(SLOTS)[None, :] < counts[0, 0][:, None]
    first_col = runs[0, 0][:, :, 0, :]
    run_len = runs[0, 0][:, :, 1, :]
    columns = jnp.arange(TILE)
    observed = (
        (columns[None, None, None, :] - first_col[:, :, :, None]) % TILE < run_len[:, :, :, None]
    ) & slot_live[:, :, None, None]
    selector = (user_tile[0, 0][:, :, None] == jnp.arange(UT)[None, None, :]).astype(jnp.bfloat16)
    values = ratings[0, 0]

    def group_terms(span, gathered, with_values):
        rows_part = gathered
        rows_part = rows_part.reshape(span, UT, TILE, rows_part.shape[-1])
        picked = jnp.einsum(
            "gsu,guar->gsar", selector, rows_part, preferred_element_type=jnp.float32
        ).astype(jnp.bfloat16)
        scores = jnp.einsum("gsar,gscr->gsac", picked, products, preferred_element_type=jnp.float32)
        if with_values:
            scores = values.astype(jnp.float32) - scores
        weights = jnp.where(observed, scores, 0.0).astype(jnp.bfloat16)
        rows_out = jnp.einsum(
            "gsac,gscr->gsar", weights, products, preferred_element_type=jnp.float32
        )
        summed = jnp.einsum("gsu,gsar->guar", selector.astype(jnp.float32), rows_out)
        return summed.reshape(span * group_rows, summed.shape[-1])

    def make_summand(gathered, with_values):
        whole = lax.axis_size("loop") * group_rows // group_rows
        extra = 0
        span = min(groups, whole + extra)
        result = group_terms(span, gathered, with_values)
        return result

    def data_part(vector, with_values):
        halves = vector.astype(jnp.bfloat16)
        grouped = lax.all_gather(halves, "own", axis=0, tiled=True)
        gathered = lax.all_gather(grouped, "loop", axis=0, tiled=True)
        loop_sums = lax.psum_scatter(
            make_summand(gathered, with_values), "loop", scatter_dimension=0, tiled=True
        )
        return lax.psum_scatter(loop_sums, "own", scatter_dimension=0, tiled=True)

    def global_sum(value):
        return lax.psum(value, ("loop", "own"))

    weight_rows = activity[:, None]
    solution = factor_start
    residual = weight_rows * data_part(solution, True) - ridge * solution
    direction = residual
    norm_now = global_sum(jnp.sum(residual * residual))
    for iteration in range(ITERS):
        image = weight_rows * data_part(direction, False) + ridge * direction
        step_size = norm_now / global_sum(jnp.sum(direction * image))
        solution = solution + step_size * direction
        residual = residual - step_size * image
        if iteration + 1 < ITERS:
            norm_next = global_sum(jnp.sum(residual * residual))
            direction = residual + norm_next / norm_now * direction
            norm_now = norm_next
    return (solution, residual)


def solution(mesh):
    placed = (
        P(("loop", "own"), None),
        P(("loop", "own")),
        P("loop", None, None, None),
        P(),
        P("loop", "own", None, None, None, None),
        P("loop", "own", None, None),
        P("loop", "own", None, None),
        P("loop", "own", None, None),
        P("loop", "own", None),
        P("loop", "own", None, None, None, None),
    )
    return jax.shard_map(
        on_device,
        mesh=mesh,
        in_specs=placed,
        out_specs=(P(("loop", "own"), None), P(("loop", "own"), None)),
        check_vma=False,
    )
```

profile of v0, /device:TPU:1, one launch (start us, length us, event | category | flops | bytes accessed | tf_op | source)
XLA Modules:
  0.0 1276.5 jit_solution(4140988907751638471)
XLA Ops:
  8.0 31.1 %all_gather.18 = bf16[256,128]{1,0:T(8,128)(2,1)} all-gather(bf16[32,128]{1,0:T(8,128)(2,1)S(1)} %convert_element_type.53), channel_id=1, replica_groups=mesh['loop'=32,'own'=8] {'own'}, dimensions={0}, use_global_device_ids=true | all-gather | bytes 73728 | tf_op jit(solution)/shard_map/all_gather | solution.py:69
  42.6 9.6 gather_fusion
  52.5 60.3 %all-gather.4.cloned.1.call-done = bf16[8192,128]{1,0:T(8,128)(2,1)} async-done(((bf16[256,128]{1,0:T(8,128)(2,1)}), bf16[8192,128]{1,0:T(8,128)(2,1)}) %all-gather.4.cloned.1.call-update) | async-done | bytes 2097168 | tf_op jit(solution)/shard_map/all_gather | solution.py:70
  112.8 7.2 fusion.38
  120.0 23.6 %fusion.22 = bf16[32,8,128,128]{3,2,1,0:T(8,128)(2,1)} fusion(bf16[32,8,128,128]{3,1,2,0:T(8,128)(2,1)} %fusion.38, bf16[1,1,32,8,128,128]{5,4,3,2,1,0:T(8,128)(2,1)} %param.14, bf16[32,8,128,128]{3,2,1,0:T(8,128)(2,1)} %bitcast.53, f32[32,8,128]{2,1,0:T(8,128)S(1)} %bitcast_convert_fusion, s32[32,8,128]{2,1,0:T(8,128)S(1)} %bitcast.63, ...), kind=kOutput, calls=%fused_computation.32 | convolution fusion | flops 2248146944 | bytes 33947904 | tf_op jit(solution)/shard_map/gsac,gscr->gsar/dot_general | solution.py:54
  143.6 8.8 fusion.9
  152.4 2.5 copy.16
  155.0 120.7 %reduce-scatter.7.cloned.1.call-done = f32[256,128]{1,0:T(8,128)} async-done(((f32[8192,128]{1,0:T(8,128)}), f32[256,128]{1,0:T(8,128)}) %reduce-scatter.7.cloned.1.call-update) | async-done | bytes 131088 | tf_op jit(solution)/shard_map/reduce_scatter | solution.py:71
  275.8 78.9 %reduce-scatter.9.cloned.1.call-done = f32[32,128]{1,0:T(8,128)} async-done(((f32[256,128]{1,0:T(8,128)}), f32[32,128]{1,0:T(8,128)}) %reduce-scatter.9.cloned.1.call-update) | async-done | bytes 16400 | tf_op jit(solution)/shard_map/reduce_scatter | solution.py:74
  355.5 30.0 %all_gather.20 = bf16[256,128]{1,0:T(8,128)(2,1)} all-gather(bf16[32,128]{1,0:T(8,128)(2,1)S(1)} %get-tuple-element.6), channel_id=1, replica_groups=mesh['loop'=32,'own'=8] {'own'}, dimensions={0}, use_global_device_ids=true | all-gather | bytes 73728 | tf_op jit(solution)/shard_map/all_gather | solution.py:69
  385.6 71.8 %all-gather.6.cloned.1.call-done = bf16[8192,128]{1,0:T(8,128)(2,1)} async-done(((bf16[256,128]{1,0:T(8,128)(2,1)}), bf16[8192,128]{1,0:T(8,128)(2,1)}) %all-gather.6.cloned.1.call-update) | async-done | bytes 2097168 | tf_op jit(solution)/shard_map/all_gather | solution.py:70
  457.4 7.4 fusion.36
  464.7 19.8 %fusion.15 = bf16[32,8,128,128]{3,2,1,0:T(8,128)(2,1)} fusion(bf16[32,8,128,128]{3,1,2,0:T(8,128)(2,1)} %fusion.36, bf16[32,8,128,128]{3,2,1,0:T(8,128)(2,1)} %bitcast.54, f32[32,8,128]{2,1,0:T(8,128)S(1)} %bitcast_convert_fusion, s32[32,8,128]{2,1,0:T(8,128)S(1)} %bitcast.64, s32[32,8,128]{2,1,0:T(8,128)S(1)} %bitcast.61, ...), kind=kOutput, calls=%fused_computation.27 | convolution fusion | flops 2239758336 | bytes 25559296 | tf_op jit(solution)/shard_map/gsac,gscr->gsar/dot_general | solution.py:54
  484.5 8.8 fusion.7
  493.4 2.5 copy.17
  496.0 120.6 %reduce-scatter.11.cloned.1.call-done = f32[256,128]{1,0:T(8,128)} async-done(((f32[8192,128]{1,0:T(8,128)}), f32[256,128]{1,0:T(8,128)}) %reduce-scatter.11.cloned.1.call-update) | async-done | bytes 131088 | tf_op jit(solution)/shard_map/reduce_scatter | solution.py:71
  616.6 79.0 %reduce-scatter.13.cloned.1.call-done = f32[32,128]{1,0:T(8,128)} async-done(((f32[256,128]{1,0:T(8,128)}), f32[32,128]{1,0:T(8,128)}) %reduce-scatter.13.cloned.1.call-update) | async-done | bytes 16400 | tf_op jit(solution)/shard_map/reduce_scatter | solution.py:74
  695.6 1.4 multiply_reduce_fusion.2
  697.0 77.5 %all-reduce = (f32[]{:T(128)}, f32[]{:T(128)}) all-reduce(f32[]{:T(128)} %get-tuple-element.3, f32[]{:T(128)} %get-tuple-element.2), channel_id=1, replica_groups=mesh['loop'=32,'own'=8] {'loop','own'}, use_global_device_ids=true, to_apply=%region_3.4 | all-reduce | flops 2 | bytes 16 | tf_op jit(solution)/shard_map/psum | solution.py:77
  775.8 1.4 multiply_reduce_fusion.1
  777.2 73.6 %psum.30 = f32[]{:T(128)} all-reduce(f32[]{:T(128)} %multiply_reduce_fusion.1), channel_id=1, replica_groups=mesh['loop'=32,'own'=8] {'loop','own'}, use_global_device_ids=true, to_apply=%region_9.10 | all-reduce | flops 1 | bytes 8 | tf_op jit(solution)/shard_map/psum | solution.py:77
  852.9 30.0 %all_gather.22 = bf16[256,128]{1,0:T(8,128)(2,1)} all-gather(bf16[32,128]{1,0:T(8,128)(2,1)S(1)} %fusion.55), channel_id=1, replica_groups=mesh['loop'=32,'own'=8] {'own'}, dimensions={0}, use_global_device_ids=true | all-gather | bytes 73728 | tf_op jit(solution)/shard_map/all_gather | solution.py:69
  883.0 66.7 %all-gather.8.cloned.1.call-done = bf16[8192,128]{1,0:T(8,128)(2,1)} async-done(((bf16[256,128]{1,0:T(8,128)(2,1)}), bf16[8192,128]{1,0:T(8,128)(2,1)}) %all-gather.8.cloned.1.call-update) | async-done | bytes 2097168 | tf_op jit(solution)/shard_map/all_gather | solution.py:70
  949.7 7.2 fusion.34
  957.0 19.8 %fusion.18 = bf16[32,8,128,128]{3,2,1,0:T(8,128)(2,1)} fusion(bf16[32,8,128,128]{3,1,2,0:T(8,128)(2,1)} %fusion.34, bf16[32,8,128,128]{3,2,1,0:T(8,128)(2,1)} %bitcast.55, f32[32,8,128]{2,1,0:T(8,128)S(1)} %bitcast_convert_fusion, s32[32,8,128]{2,1,0:T(8,128)S(1)} %bitcast.65, s32[32,8,128]{2,1,0:T(8,128)S(1)} %bitcast.62, ...), kind=kOutput, calls=%fused_computation.29 | convolution fusion | flops 2239758336 | bytes 25559296 | tf_op jit(solution)/shard_map/gsac,gscr->gsar/dot_general | solution.py:54
  976.7 8.9 fusion.5
  985.6 2.5 copy.18
  988.2 120.6 %reduce-scatter.15.cloned.1.call-done = f32[256,128]{1,0:T(8,128)} async-done(((f32[8192,128]{1,0:T(8,128)}), f32[256,128]{1,0:T(8,128)}) %reduce-scatter.15.cloned.1.call-update) | async-done | bytes 131088 | tf_op jit(solution)/shard_map/reduce_scatter | solution.py:71
  1108.9 79.3 %reduce-scatter.17.cloned.1.call-done = f32[32,128]{1,0:T(8,128)} async-done(((f32[256,128]{1,0:T(8,128)}), f32[32,128]{1,0:T(8,128)}) %reduce-scatter.17.cloned.1.call-update) | async-done | bytes 16400 | tf_op jit(solution)/shard_map/reduce_scatter | solution.py:74
  1188.2 1.4 multiply_reduce_fusion
  1189.6 77.3 %psum.31 = f32[]{:T(128)} all-reduce(f32[]{:T(128)} %multiply_reduce_fusion), channel_id=1, replica_groups=mesh['loop'=32,'own'=8] {'loop','own'}, use_global_device_ids=true, to_apply=%region_13.14 | all-reduce | flops 1 | bytes 8 | tf_op jit(solution)/shard_map/psum | solution.py:77
  1268.3 1.4 multiply_subtract_fusion
  (48 shorter events, 6.6 us)
Async XLA Ops:
  7.2 34.5 %copy-start = (bf16[2048,128]{1,0:T(8,128)(2,1)S(1)}, bf16[2048,128]{1,0:T(8,128)(2,1)}, u32[]{:S(2)}) copy-start(bf16[2048,128]{1,0:T(8,128)(2,1)} %param.13) | copy-start | bytes 1572868
  7.2 105.6 %all-gather.4.cloned.1.call-start = ((), (), s32[]{:S(2)}) async-start(), calls=%async_computation.6 | async-start | bytes 2162688 | tf_op jit(solution)/shard_map/all_gather | solution.py:70
  39.2 236.6 %reduce-scatter.7.cloned.1.call-start = ((), (), s32[]{:S(2)}) async-start(), calls=%async_computation.7 | async-start | bytes 4325376 | tf_op jit(solution)/shard_map/reduce_scatter | solution.py:71
  42.6 9.6 copy-start.6
  42.6 9.7 copy-start.3
  152.4 202.3 %copy-start.4 = (f32[32,128]{1,0:T(8,128)S(1)}, f32[32,128]{1,0:T(8,128)}, u32[]{:S(2)}) copy-start(f32[32,128]{1,0:T(8,128)} %param.10) | copy-start | bytes 49156
  152.4 202.3 %copy-start.5 = (f32[32]{0:T(128)S(1)}, f32[32]{0:T(128)}, u32[]{:S(2)}) copy-start(f32[32]{0:T(128)} %param.11) | copy-start | bytes 388
  155.0 199.7 %reduce-scatter.9.cloned.1.call-start = ((), (), s32[]{:S(2)}) async-start(), calls=%async_computation.8 | async-start | bytes 147456 | tf_op jit(solution)/shard_map/reduce_scatter | solution.py:74
  275.8 181.6 %all-gather.6.cloned.1.call-start = ((), (), s32[]{:S(2)}) async-start(), calls=%async_computation.9 | async-start | bytes 2162688 | tf_op jit(solution)/shard_map/all_gather | solution.py:70
  385.5 231.0 %reduce-scatter.11.cloned.1.call-start = ((), (), s32[]{:S(2)}) async-start(), calls=%async_computation.10 | async-start | bytes 4325376 | tf_op jit(solution)/shard_map/reduce_scatter | solution.py:71
  495.9 199.7 %reduce-scatter.13.cloned.1.call-start = ((), (), s32[]{:S(2)}) async-start(), calls=%async_computation.11 | async-start | bytes 147456 | tf_op jit(solution)/shard_map/reduce_scatter | solution.py:74
  616.6 333.2 %all-gather.8.cloned.1.call-start = ((), (), s32[]{:S(2)}) async-start(), calls=%async_computation.12 | async-start | bytes 2162688 | tf_op jit(solution)/shard_map/all_gather | solution.py:70
  883.0 225.9 %reduce-scatter.15.cloned.1.call-start = ((), (), s32[]{:S(2)}) async-start(), calls=%async_computation.13 | async-start | bytes 4325376 | tf_op jit(solution)/shard_map/reduce_scatter | solution.py:71
  976.7 293.0 %copy-start.1 = (bf16[2048,128]{1,0:T(8,128)(2,1)S(1)}, bf16[2048,128]{1,0:T(8,128)(2,1)}, u32[]{:S(2)}) copy-start(bf16[2048,128]{1,0:T(8,128)(2,1)} %param.13) | copy-start | bytes 1572868
  985.6 202.6 %copy-start.2 = (f32[32,128]{1,0:T(8,128)S(1)}, f32[32,128]{1,0:T(8,128)}, u32[]{:S(2)}) copy-start(f32[32,128]{1,0:T(8,128)} %reduce-scatter.13.cloned.1.call-done) | copy-start | bytes 49156
  988.2 200.0 %reduce-scatter.17.cloned.1.call-start = ((), (), s32[]{:S(2)}) async-start(), calls=%async_computation.14 | async-start | bytes 147456 | tf_op jit(solution)/shard_map/reduce_scatter | solution.py:74
Sparse Core Ops, SparseCore 0:
  39.3 73.4 all-gather.3
  155.1 120.5 reduce-scatter.6
  279.5 75.0 reduce-scatter.8
  385.6 71.6 all-gather.5
  496.1 120.4 reduce-scatter.10
  620.2 75.3 reduce-scatter.12
  883.1 66.5 all-gather.7
  988.3 120.5 reduce-scatter.14
  1112.7 75.5 reduce-scatter.16
where the time goes:
time: 1280 us
  waiting for transfers between devices  798 us (62%)
  blocking collectives  320 us (25%)
  matrix products  111 us (9%)
  local copies, waits for them, and re-layouts  19.3 us (2%)
  between operations  18.2 us (1%)
    reduce_scatter x3, waiting for transfers between devices, data_part(): lax.psum_scatter(make_summand(gathered, with_values), 'loop', scatter_dim...  362 us
    reduce_scatter x3, waiting for transfers between devices, data_part(): return lax.psum_scatter(loop_sums, 'own', scatter_dimension=0, tiled=True)  237 us
    psum x3, blocking collectives, global_sum(): return lax.psum(value, ('loop', 'own'))  228 us
    all_gather x3, waiting for transfers between devices, data_part(): gathered = lax.all_gather(grouped, 'loop', axis=0, tiled=True)  199 us
    all_gather x3, blocking collectives, data_part(): grouped = lax.all_gather(halves, 'own', axis=0, tiled=True)  91.2 us
    dot_general x3, matrix products, group_terms(): jnp.einsum('gsac,gscr->gsar', weights, products, preferred_element_type=j...  63.1 us
    dot_general x3, matrix products, group_terms(): jnp.einsum('gsu,gsar->guar', selector.astype(jnp.float32), rows_out)  26.6 us
  transfers between devices with their start and end apart: 9, of which 9 were waited for; matrix products, arithmetic and copies ran while one was open for 1% of the time, Pallas kernels for 0%

commit v1 on v0

v1 whole, which is shorter than its diff:
```python
import functools

import jax
import jax.numpy as jnp
from jax import lax
from jax.experimental import pallas as pl
from jax.experimental.pallas import tpu as pltpu
from jax.sharding import PartitionSpec as P

TILE = 128
R = 128
UT = 2
SLOTS = 8
GROUPS = 32
WB = 8
NP = 4
NQ = 4
NZ = 8
ROWS = 32
STEP_GROUPS = 4
RIDGE = 0.05
MESH = pl.DeviceIdType.MESH
F32 = jnp.float32
BF16 = jnp.bfloat16
VMEM = pl.BlockSpec(memory_space=pltpu.VMEM)


def place():
    loop = lax.axis_index("loop")
    own = lax.axis_index("own")
    c = loop % 2
    x = (own // 4) * 2 + (loop // 2) % 2
    y = own % 4
    z = loop // 4
    return c, x * (1 - c) + y * c, y * (1 - c) + x * c, z


def device(c, p, q, z):
    x = p * (1 - c) + q * c
    y = q * (1 - c) + p * c
    return {"loop": (z * 2 + x % 2) * 2 + c, "own": (x // 2) * 4 + y}


def send(src, dst, sems, k, to):
    copy = pltpu.make_async_remote_copy(
        src_ref=src,
        dst_ref=dst,
        send_sem=sems.at[0, k],
        recv_sem=sems.at[1, k],
        device_id=to,
        device_id_type=MESH,
    )
    copy.start()
    return copy


def enter(here):
    c, p, q, z = here
    barrier = pltpu.get_barrier_semaphore()
    partners = [device(1 - c, q, p, z)]
    partners += [device(c, (p + k) % NP, q, z) for k in range(1, NP)]
    partners += [device(c, p, (q + k) % NQ, z) for k in range(1, NQ)]
    partners += [device(c, p, q, (z + k) % NZ) for k in range(1, NZ)]
    for partner in partners:
        pl.semaphore_signal(barrier, inc=1, device_id=partner, device_id_type=MESH)
    pl.semaphore_wait(barrier, len(partners))


def reduce_scatter(here, part, core_in, p_out, p_in, q_out, q_in, z_out, z_in, c_sem, p_sem, q_sem, z_sem):
    c, p, q, z = here
    copies = []
    core = {}
    for k in (1, 2, 3, 0):
        pp = (q + k) % NP
        core[k] = send(part.at[1 - c, pp], core_in.at[pp], c_sem, k, device(1 - c, q, p, z))
        copies.append(core[k])
    ring = {}
    for k in range(1, NP):
        pp = (p + k) % NP
        core[k].wait_recv()

        def to_send(i, carry):
            p_out[k - 1, i] = (part[c, pp, i] + core_in[pp, i]).astype(BF16)
            return carry

        lax.fori_loop(0, NQ, to_send, 0)
        ring[k] = send(p_out.at[k - 1], p_in.at[k - 1], p_sem, k, device(c, pp, q, z))
        copies.append(ring[k])
    core[0].wait_recv()
    for k in range(1, NP):
        ring[k].wait_recv()

    def chunk(qq):
        total = part[c, p, qq] + core_in[p, qq]
        for k in range(1, NP):
            total = total + p_in[k - 1, qq].astype(F32)
        return total

    ring = {}
    for k in range(1, NQ):
        qq = (q + k) % NQ
        q_out[k - 1] = chunk(qq).astype(BF16)
        ring[k] = send(q_out.at[k - 1], q_in.at[k - 1], q_sem, k, device(c, p, qq, z))
        copies.append(ring[k])
    total = chunk(q)
    for k in range(1, NQ):
        ring[k].wait_recv()
        total = total + q_in[k - 1].astype(F32)
    z_out[...] = total
    ring = {}
    for k in range(1, NZ):
        zz = (z + k) % NZ
        ring[k] = send(z_out.at[zz], z_in.at[k - 1], z_sem, k, device(c, p, q, zz))
        copies.append(ring[k])
    rows = z_out[z]
    for k in range(1, NZ):
        ring[k].wait_recv()
        rows = rows + z_in[k - 1]
    for copy in copies:
        copy.wait_send()
    return rows


class Sum:
    def __init__(self, here, refs):
        self.here = here
        self.slots, self.sems = refs
        self.copies = []

    def start(self, stage, tile):
        c, p, q, z = self.here
        slots, sems = self.slots, self.sems
        place_in, to, base = {
            "z": (z, [device(c, p, q, (z + k) % NZ) for k in range(1, NZ)], 0),
            "q": (q, [device(c, p, (q + k) % NQ, z) for k in range(1, NQ)], 8),
            "p": (p, [device(c, (p + k) % NP, q, z) for k in range(1, NP)], 12),
            "c": (c, [device(1 - c, q, p, z)], 16),
        }[stage]
        self.base, self.size = base, len(to) + 1
        mine = slots.at[base + place_in]
        mine[...] = tile
        self.now = [send(mine, mine, sems, base + k, d) for k, d in enumerate(to)]
        self.copies += self.now

    def finish(self):
        for copy in self.now:
            copy.wait_recv()
        total = self.slots[self.base]
        for k in range(1, self.size):
            total = total + self.slots[self.base + k]
        return total

    def close(self):
        for copy in self.copies:
            copy.wait_send()

    def whole(self, tile):
        for stage in ("z", "q", "p", "c"):
            self.start(stage, tile)
            tile = self.finish()
        self.close()
        return tile


def gather(here, rows, out, sems, total=None, tile=None):
    c, p, q, z = here
    c_sem, p_sem, q_sem, z_sem = sems
    copies = []

    def note(stage, value):
        if total is not None:
            total.start(stage, value)

    out[c, p, q, z] = rows.astype(BF16)
    mine = out.at[c, p, q, z]
    ring = [send(mine, mine, z_sem, k, device(c, p, q, (z + k) % NZ)) for k in range(1, NZ)]
    note("z", tile)
    for copy in ring:
        copy.wait_recv()
    copies += ring
    mine = out.at[c, p, q]
    ring = [send(mine, mine, q_sem, k, device(c, p, (q + k) % NQ, z)) for k in range(1, NQ)]
    if total is not None:
        note("q", total.finish())
    for copy in ring:
        copy.wait_recv()
    copies += ring
    mine = out.at[c, p]
    ring = [send(mine, mine, p_sem, k, device(c, (p + k) % NP, q, z)) for k in range(1, NP)]
    copies += ring
    other = device(1 - c, q, p, z)
    core = [send(mine, mine, c_sem, 0, other)]
    if total is not None:
        note("p", total.finish())
    for k, copy in enumerate(ring, 1):
        copy.wait_recv()
        arrived = out.at[c, (p - k + NP) % NP]
        core.append(send(arrived, arrived, c_sem, k, other))
    if total is not None:
        note("c", total.finish())
        tile = total.finish()
        total.close()
    for copy in core:
        copy.wait_recv()
    for copy in copies + core:
        copy.wait_send()
    return tile


def folded(values):
    tile = values[0:8]
    for k in range(1, ROWS // 8):
        tile = tile + values[8 * k : 8 * k + 8]
    return tile


def all_of(tile):
    return jnp.sum(tile, keepdims=True)


SCATTER_SCRATCH = [
    pltpu.VMEM((NP, NQ, NZ, ROWS, R), F32),
    pltpu.VMEM((NP - 1, NQ, NZ, ROWS, R), BF16),
    pltpu.VMEM((NP - 1, NQ, NZ, ROWS, R), BF16),
    pltpu.VMEM((NQ - 1, NZ, ROWS, R), BF16),
    pltpu.VMEM((NQ - 1, NZ, ROWS, R), BF16),
    pltpu.VMEM((NZ, ROWS, R), F32),
    pltpu.VMEM((NZ - 1, ROWS, R), F32),
    pltpu.SemaphoreType.DMA((2, NP)),
    pltpu.SemaphoreType.DMA((2, NP)),
    pltpu.SemaphoreType.DMA((2, NQ)),
    pltpu.SemaphoreType.DMA((2, NZ)),
]
GATHER_SCRATCH = [
    pltpu.SemaphoreType.DMA((2, NP)),
    pltpu.SemaphoreType.DMA((2, NP)),
    pltpu.SemaphoreType.DMA((2, NQ)),
    pltpu.SemaphoreType.DMA((2, NZ)),
]
SUM_SCRATCH = [pltpu.VMEM((18, 8, R), F32), pltpu.SemaphoreType.DMA((2, 17))]
N_S, N_G, N_SUM = len(SCATTER_SCRATCH), len(GATHER_SCRATCH), len(SUM_SCRATCH)

BLOCK = jax.ShapeDtypeStruct((ROWS, R), F32)
SCALAR = jax.ShapeDtypeStruct((8, R), F32)
WHOLE = jax.ShapeDtypeStruct((2, NP, NQ, NZ, ROWS, R), BF16)


def communicate(kernel, number, outs, scratch, *args):
    return pl.pallas_call(
        kernel,
        out_shape=outs,
        in_specs=[VMEM] * len(args),
        out_specs=[VMEM] * len(outs),
        scratch_shapes=scratch,
        compiler_params=pltpu.CompilerParams(collective_id=number, has_side_effects=True),
        name=f"comm{number}",
    )(*args)


def first_kernel(start, out, *scratch):
    here = place()
    enter(here)
    gather(here, start[...], out, scratch)


def residual_kernel(part, start, activity, residual, square, out, *scratch):
    here = place()
    enter(here)
    rows = reduce_scatter(here, part, *scratch[:N_S])
    r = activity[...] * rows - RIDGE * start[...]
    residual[...] = r
    total = Sum(here, scratch[N_S + N_G :])
    square[...] = gather(here, r, out, scratch[N_S : N_S + N_G], total, folded(r * r))


def step_kernel(part, start, activity, residual, square, solution, later, image, new, out, *scratch):
    here = place()
    enter(here)
    rows = reduce_scatter(here, part, *scratch[:N_S])
    r = residual[...]
    q = activity[...] * rows + RIDGE * r
    image[...] = q
    at = N_S + N_G
    along = Sum(here, scratch[at : at + N_SUM]).whole(folded(r * q))
    step = all_of(square[...]) / all_of(along)
    solution[...] = start[...] + step * r
    r = r - step * q
    later[...] = r
    total = Sum(here, scratch[at + N_SUM :])
    new[...] = gather(here, r, out, scratch[N_S:at], total, folded(r * r))


def last_kernel(part, activity, before, residual, square, image, new, solution, out, left, *scratch):
    here = place()
    enter(here)
    rows = reduce_scatter(here, part, *scratch[:N_S])
    r = residual[...]
    rr = all_of(new[...])
    ratio = rr / all_of(square[...])
    d = r + ratio * before[...]
    q = activity[...] * rows + RIDGE * r + ratio * image[...]
    along = Sum(here, scratch[N_S:]).whole(folded(d * q))
    step = rr / all_of(along)
    out[...] = solution[...] + step * d
    left[...] = r - step * q


def blocks_kernel(first, user_tile, word_tile, counts, *refs):
    if first:
        whole, words, subs, runs, ratings, part, mask = refs
    else:
        whole, words, subs, mask, part = refs
    step = pl.program_id(0)
    columns = lax.broadcasted_iota(jnp.int32, (TILE, TILE), 1)

    def group(i, carry):
        g = step * STEP_GROUPS + i
        c, xl, z = g % 2, (g // 2) % 2, g // 4
        by_x, by_y = 32 - 24 * c, 8 + 24 * c
        base = c * 128 + xl * by_x + z
        for u in range(UT):
            for y in range(4):
                part[base + 2 * u * by_x + y * by_y] = jnp.zeros((ROWS, R), F32)
        sub_rows = subs[i]
        if first:
            run = runs[i]

        def half(slots):
            for s in slots:
                b = g * SLOTS + s
                at = base + user_tile[b] * (2 * by_x)
                rows = jnp.concatenate([whole[at + y * by_y] for y in range(4)], axis=0)
                word = words[word_tile[b]].astype(F32)
                products = (word * sub_rows[s : s + 1]).astype(BF16)
                scores = lax.dot_general(rows, products, (((1,), (1,)), ((), ())), preferred_element_type=F32)
                if first:
                    scores = ratings[i, s].astype(F32) - scores
                    seen = ((columns - run[:, 2 * s : 2 * s + 1]) & (TILE - 1)) < run[:, 2 * s + 1 : 2 * s + 2]
                    seen = jnp.where(seen, 1.0, 0.0)
                    mask[i, s] = seen.astype(BF16)
                    weights = (scores * seen).astype(BF16)
                else:
                    weights = scores.astype(BF16) * mask[i, s]
                added = jnp.dot(weights, products, preferred_element_type=F32)
                for y in range(4):
                    part[at + y * by_y] += added[ROWS * y : ROWS * y + ROWS]

        half(range(4))

        @pl.when(counts[g] > 4)
        def _():
            half(range(4, SLOTS))

        return carry

    lax.fori_loop(0, STEP_GROUPS, group, 0)


def block_sums(tables, whole, words, subs, runs=None, ratings=None, mask=None):
    first = mask is None
    flat = (2 * NP * NQ * NZ, ROWS, R)

    def resident(*shape):
        return pl.BlockSpec(shape, lambda i, *_: (0,) * len(shape))

    def streamed(*shape):
        return pl.BlockSpec((STEP_GROUPS,) + shape, lambda i, *_: (i,) + (0,) * len(shape))

    blocks = streamed(SLOTS, TILE, TILE)
    in_specs = [resident(*flat), resident(WB, TILE, R), streamed(SLOTS, R)]
    out_specs = [resident(*flat)]
    out_shape = [jax.ShapeDtypeStruct(flat, F32)]
    if first:
        in_specs += [streamed(TILE, 2 * SLOTS), blocks]
        out_specs += [blocks]
        out_shape += [jax.ShapeDtypeStruct((GROUPS, SLOTS, TILE, TILE), BF16)]
        args = (runs, ratings)
    else:
        in_specs += [blocks]
        args = (mask,)
    result = pl.pallas_call(
        functools.partial(blocks_kernel, first),
        out_shape=out_shape,
        grid_spec=pltpu.PrefetchScalarGridSpec(
            num_scalar_prefetch=len(tables),
            grid=(GROUPS // STEP_GROUPS,),
            in_specs=in_specs,
            out_specs=out_specs,
        ),
        compiler_params=pltpu.CompilerParams(dimension_semantics=("arbitrary",)),
        name="blocks_first" if first else "blocks_next",
    )(*tables, whole.reshape(flat), words, subs, *args)
    part = result[0].reshape(2, NP, NQ, NZ, ROWS, R)
    return (part, result[1]) if first else part


def on_device(
    factor_start,
    activity,
    word_factors,
    sub_factors,
    ratings,
    user_tile,
    word_tile,
    subreddit,
    counts,
    runs,
):
    live = counts[0, 0]
    tables = (user_tile[0, 0].reshape(-1), word_tile[0, 0].reshape(-1), live)
    words = word_factors[0]
    subs = sub_factors[subreddit[0, 0]].astype(F32)
    used = jnp.arange(SLOTS)[None, :] < live[:, None]
    lengths = jnp.where(used[:, :, None], runs[0, 0][:, :, 1, :], 0)
    run = jnp.stack([runs[0, 0][:, :, 0, :], lengths], axis=2)
    run = run.reshape(GROUPS, 2 * SLOTS, TILE).transpose(0, 2, 1)
    scale = jnp.broadcast_to(activity[:, None], (ROWS, R))

    (whole,) = communicate(first_kernel, 0, [WHOLE], GATHER_SCRATCH, factor_start)
    part, mask = block_sums(tables, whole, words, subs, runs=run, ratings=ratings[0, 0])
    scratch = SCATTER_SCRATCH + GATHER_SCRATCH
    residual, square, whole = communicate(
        residual_kernel, 1, [BLOCK, SCALAR, WHOLE], scratch + SUM_SCRATCH, part, factor_start, scale
    )
    part = block_sums(tables, whole, words, subs, mask=mask)
    solution, later, image, new, whole = communicate(
        step_kernel,
        2,
        [BLOCK, BLOCK, BLOCK, SCALAR, WHOLE],
        scratch + SUM_SCRATCH + SUM_SCRATCH,
        part,
        factor_start,
        scale,
        residual,
        square,
    )
    part = block_sums(tables, whole, words, subs, mask=mask)
    return tuple(
        communicate(
            last_kernel,
            3,
            [BLOCK, BLOCK],
            SCATTER_SCRATCH + SUM_SCRATCH,
            part,
            scale,
            residual,
            later,
            square,
            image,
            new,
            solution,
        )
    )


def solution(mesh):
    placed = (
        P(("loop", "own"), None),
        P(("loop", "own")),
        P("loop", None, None, None),
        P(),
        P("loop", "own", None, None, None, None),
        P("loop", "own", None, None),
        P("loop", "own", None, None),
        P("loop", "own", None, None),
        P("loop", "own", None),
        P("loop", "own", None, None, None, None),
    )
    return jax.shard_map(
        on_device,
        mesh=mesh,
        in_specs=placed,
        out_specs=(P(("loop", "own"), None), P(("loop", "own"), None)),
        check_vma=False,
    )
```

time: 1280 us -> 332 us (0.26)
  waiting for transfers between devices: 798 us -> 0 us
  Pallas kernels: 0 us -> 323 us
  blocking collectives: 320 us -> 0 us
  matrix products: 111 us -> 0 us
  between operations: 18.2 us -> 0.73 us
    reduce_scatter x6 -> x0, waiting for transfers between devices: 599 us -> none  [the longest x3 362 us: data_part(): lax.psum_scatter(make_summand(gathered, with_values), 'loop', scatter_dim...]
    pallas_call x0 -> x7, Pallas kernels: none -> 323 us  [the longest x4 196 us: communicate(): pl.pallas_call(kernel, out_shape=outs, in_specs=[VMEM] * len(args), out_s...]
    psum x3 -> x0, blocking collectives: 228 us -> none  [global_sum(): return lax.psum(value, ('loop', 'own'))]
    all_gather x3 -> x0, waiting for transfers between devices: 199 us -> none  [data_part(): gathered = lax.all_gather(grouped, 'loop', axis=0, tiled=True)]
    dot_general x9 -> x0, matrix products: 111 us -> none  [the longest x3 63.1 us: group_terms(): jnp.einsum('gsac,gscr->gsar', weights, products, preferred_element_type=j...]
    all_gather x3 -> x0, blocking collectives: 91.2 us -> none  [data_part(): grouped = lax.all_gather(halves, 'own', axis=0, tiled=True)]
  transfers between devices with their start and end apart: 9 -> 0, of which waited for: 9 -> 0; matrix products, arithmetic and copies ran while one was open for 1% -> 0% of each run, Pallas kernels for 0% -> 0%
where the time goes in v1:
time: 332 us; the launch traced here: 335 us
  Pallas kernels  323 us (97%)
  local copies, waits for them, and re-layouts  8.82 us (3%)
    pallas_call x4, Pallas kernels, communicate(): pl.pallas_call(kernel, out_shape=outs, in_specs=[VMEM] * len(args), out_s...  196 us
    pallas_call x3, Pallas kernels, block_sums(): pl.pallas_call(functools.partial(blocks_kernel, first), out_shape=out_sha...  127 us

profile of v1, /device:TPU:1, one launch (start us, length us, event | category | flops | bytes accessed | tf_op | source)
XLA Modules:
  0.0 334.7 jit_solution(8353557270541567279)
XLA Ops:
  0.6 0.0 copy-start
  0.6 0.0 copy-start.1
  0.7 0.0 copy-start.2
  0.7 0.7 iota_compare_fusion
  1.4 1.0 copy.19
  2.4 0.1 fusion
  2.6 1.9 copy.17
  4.5 0.7 compare_select_fusion
  5.2 0.1 copy.15
  5.3 0.1 reshape.87
  5.4 0.0 copy-done
  5.4 0.9 gather_fusion
  6.2 0.7 bitcast_convert_fusion.refs_2_
  6.9 0.0 copy-done.1
  6.9 0.1 copy.13
  7.0 0.7 reshape_squeeze.6.user_tile
  7.6 0.0 copy-done.2
  7.6 0.1 copy.14
  7.7 0.7 reshape_squeeze.7.word_tile
  8.4 32.7 %comm0.1 = bf16[2,4,4,8,32,128]{5,4,3,2,1,0:T(8,128)(2,1)} custom-call(f32[32,128]{1,0:T(8,128)} %start.5), custom_call_target="tpu_custom_call" | custom-call | tf_op jit(solution)/shard_map/comm0/pallas_call | solution.py:249
  41.1 0.0 copy-start.3
  41.1 42.9 %blocks_first.1 = (f32[256,32,128]{2,1,0:T(8,128)}, bf16[32,8,128,128]{3,2,1,0:T(8,128)(2,1)}) custom-call(s32[256]{0:T(256)} %reshape_squeeze.6.user_tile, s32[256]{0:T(256)} %reshape_squeeze.7.word_tile, s32[32]{0:T(128)} %bitcast.39, bf16[256,32,128]{2,1,0:T(8,128)(2,1)} %bitcast.29, bf16[8,128,128]{2,1,0:T(8,128)(2,1)} %bitcast.31, ...), custom_call_target="tpu_custom_call" | custom-call | tf_op jit(solution)/shard_map/blocks_first/pallas_call | solution.py:381
  84.0 0.0 copy-done.3
  84.0 0.7 broadcast_in_dim.23.activity
  84.7 55.6 %comm1.1 = (f32[32,128]{1,0:T(8,128)}, f32[8,128]{1,0:T(8,128)}, bf16[2,4,4,8,32,128]{5,4,3,2,1,0:T(8,128)(2,1)}) custom-call(f32[2,4,4,8,32,128]{5,4,3,2,1,0:T(8,128)} %bitcast.30, f32[32,128]{1,0:T(8,128)} %start.5, f32[32,128]{1,0:T(8,128)} %broadcast_in_dim.23.activity), custom_call_target="tpu_custom_call" | custom-call | tf_op jit(solution)/shard_map/comm1/pallas_call | solution.py:249
  140.2 42.1 %blocks_next.2 = f32[256,32,128]{2,1,0:T(8,128)} custom-call(s32[256]{0:T(256)} %reshape_squeeze.6.user_tile, s32[256]{0:T(256)} %reshape_squeeze.7.word_tile, s32[32]{0:T(128)} %bitcast.40, bf16[256,32,128]{2,1,0:T(8,128)(2,1)} %bitcast.35, bf16[8,128,128]{2,1,0:T(8,128)(2,1)} %bitcast.32, f32[32,8,128]{2,1,0:T(8,128)} %bitcast_convert_fusion.refs_2_, ...), custom_call_target="tpu_custom_call" | custom-call | tf_op jit(solution)/shard_map/blocks_next/pallas_call | solution.py:381
  182.3 65.7 %comm2.1 = (f32[32,128]{1,0:T(8,128)}, f32[32,128]{1,0:T(8,128)}, f32[32,128]{1,0:T(8,128)}, f32[8,128]{1,0:T(8,128)}, bf16[2,4,4,8,32,128]{5,4,3,2,1,0:T(8,128)(2,1)}) custom-call(f32[2,4,4,8,32,128]{5,4,3,2,1,0:T(8,128)} %bitcast.26, f32[32,128]{1,0:T(8,128)} %start.5, f32[32,128]{1,0:T(8,128)} %broadcast_in_dim.23.activity, ...), custom_call_target="tpu_custom_call" | custom-call | tf_op jit(solution)/shard_map/comm2/pallas_call | solution.py:249
  248.0 42.1 %blocks_next.3 = f32[256,32,128]{2,1,0:T(8,128)} custom-call(s32[256]{0:T(256)} %reshape_squeeze.6.user_tile, s32[256]{0:T(256)} %reshape_squeeze.7.word_tile, s32[32]{0:T(128)} %bitcast.41, bf16[256,32,128]{2,1,0:T(8,128)(2,1)} %bitcast.34, bf16[8,128,128]{2,1,0:T(8,128)(2,1)} %bitcast.33, f32[32,8,128]{2,1,0:T(8,128)} %bitcast_convert_fusion.refs_2_, ...), custom_call_target="tpu_custom_call" | custom-call | tf_op jit(solution)/shard_map/blocks_next/pallas_call | solution.py:381
  290.0 42.0 %comm3.1 = (f32[32,128]{1,0:T(8,128)}, f32[32,128]{1,0:T(8,128)}) custom-call(f32[2,4,4,8,32,128]{5,4,3,2,1,0:T(8,128)} %bitcast.25, f32[32,128]{1,0:T(8,128)} %broadcast_in_dim.23.activity, f32[32,128]{1,0:T(8,128)} %get-tuple-element.15.residual.before, f32[32,128]{1,0:T(8,128)} %get-tuple-element.18.residual, f32[8,128]{1,0:T(8,128)} %get-tuple-element.16.square, ...), custom_call_target="tpu_custom_call" | custom-call | tf_op jit(solution)/shard_map/comm3/pallas_call | solution.py:249
  332.1 1.3 copy.22
  333.4 1.3 copy.23
  (2 shorter events, 0.0 us)
Async XLA Ops:
  0.6 4.7 %copy-start = (bf16[2048,128]{1,0:T(8,128)(2,1)S(1)}, bf16[2048,128]{1,0:T(8,128)(2,1)}, u32[]{:S(2)}) copy-start(bf16[2048,128]{1,0:T(8,128)(2,1)} %param.13) | copy-start | bytes 1572868
  0.6 6.3 %copy-start.1 = (s32[1,1,32,8]{2,3,1,0:T(8,128)S(1)}, s32[1,1,32,8]{2,3,1,0:T(8,128)}, u32[]{:S(2)}) copy-start(s32[1,1,32,8]{2,3,1,0:T(8,128)} %param.15) | copy-start | bytes 3076
  0.7 7.0 %copy-start.2 = (s32[1,1,32,8]{2,3,1,0:T(8,128)S(1)}, s32[1,1,32,8]{2,3,1,0:T(8,128)}, u32[]{:S(2)}) copy-start(s32[1,1,32,8]{2,3,1,0:T(8,128)} %param.16) | copy-start | bytes 3076
  41.1 42.9 %copy-start.3 = (f32[32]{0:T(128)S(1)}, f32[32]{0:T(128)}, u32[]{:S(2)}) copy-start(f32[32]{0:T(128)} %param.11) | copy-start | bytes 388

commit v2 on v1

--- a/solution.py
+++ b/solution.py
@@ -252,7 +252,9 @@
         in_specs=[VMEM] * len(args),
         out_specs=[VMEM] * len(outs),
         scratch_shapes=scratch,
-        compiler_params=pltpu.CompilerParams(collective_id=number, has_side_effects=True),
+        compiler_params=pltpu.CompilerParams(
+            collective_id=number, has_side_effects=True, vmem_limit_bytes=18 << 20
+        ),
         name=f"comm{number}",
     )(*args)
 
@@ -318,38 +320,45 @@
         c, xl, z = g % 2, (g // 2) % 2, g // 4
         by_x, by_y = 32 - 24 * c, 8 + 24 * c
         base = c * 128 + xl * by_x + z
-        for u in range(UT):
-            for y in range(4):
-                part[base + 2 * u * by_x + y * by_y] = jnp.zeros((ROWS, R), F32)
         sub_rows = subs[i]
         if first:
             run = runs[i]
 
         def half(slots):
+            work = []
             for s in slots:
                 b = g * SLOTS + s
-                at = base + user_tile[b] * (2 * by_x)
+                u = user_tile[b]
+                at = base + u * (2 * by_x)
                 rows = jnp.concatenate([whole[at + y * by_y] for y in range(4)], axis=0)
                 word = words[word_tile[b]].astype(F32)
                 products = (word * sub_rows[s : s + 1]).astype(BF16)
                 scores = lax.dot_general(rows, products, (((1,), (1,)), ((), ())), preferred_element_type=F32)
+                work.append((s, u, products, scores))
+            top, low = [], []
+            for s, u, products, sc in work:
                 if first:
-                    scores = ratings[i, s].astype(F32) - scores
+                    sc = ratings[i, s].astype(F32) - sc
                     seen = ((columns - run[:, 2 * s : 2 * s + 1]) & (TILE - 1)) < run[:, 2 * s + 1 : 2 * s + 2]
                     seen = jnp.where(seen, 1.0, 0.0)
                     mask[i, s] = seen.astype(BF16)
-                    weights = (scores * seen).astype(BF16)
+                    w = (sc * seen).astype(BF16)
                 else:
-                    weights = scores.astype(BF16) * mask[i, s]
-                added = jnp.dot(weights, products, preferred_element_type=F32)
+                    w = sc.astype(BF16) * mask[i, s]
+                in_low = jnp.full((TILE, TILE), u, jnp.int32).astype(F32).astype(BF16)
+                w1 = w * in_low
+                top.append(w - w1)
+                low.append(w1)
+            both = jnp.concatenate([jnp.concatenate(top, 1), jnp.concatenate(low, 1)], 0)
+            prod = jnp.concatenate([w[2] for w in work], 0)
+            added = jnp.dot(both, prod, preferred_element_type=F32)
+            for u in range(UT):
                 for y in range(4):
-                    part[at + y * by_y] += added[ROWS * y : ROWS * y + ROWS]
-
-        half(range(4))
-
-        @pl.when(counts[g] > 4)
-        def _():
-            half(range(4, SLOTS))
+                    r0 = u * TILE + ROWS * y
+                    part[base + 2 * u * by_x + y * by_y] = added[r0 : r0 + ROWS]
+
+        half(range(8))
+
 
         return carry
 
@@ -387,7 +396,9 @@
             in_specs=in_specs,
             out_specs=out_specs,
         ),
-        compiler_params=pltpu.CompilerParams(dimension_semantics=("arbitrary",)),
+        compiler_params=pltpu.CompilerParams(
+            dimension_semantics=("arbitrary",), vmem_limit_bytes=28 << 20
+        ),
         name="blocks_first" if first else "blocks_next",
     )(*tables, whole.reshape(flat), words, subs, *args)
     part = result[0].reshape(2, NP, NQ, NZ, ROWS, R)

time: 332 us -> 245 us (0.74)
  Pallas kernels: 323 us -> 234 us
    pallas_call x3, Pallas kernels: 127 us -> 54.3 us  [block_sums(): pl.pallas_call(functools.partial(blocks_kernel, first), out_shape=out_sha...]
    pallas_call x4, Pallas kernels: 196 us -> 180 us  [communicate(): pl.pallas_call(kernel, out_shape=outs, in_specs=[VMEM] * len(args), out_s...]
where the time goes in v2:
time: 245 us; the launch traced here: 244 us
  Pallas kernels  234 us (96%)
  local copies, waits for them, and re-layouts  7.71 us (3%)
    pallas_call x4, Pallas kernels, communicate(): pl.pallas_call(kernel, out_shape=outs, in_specs=[VMEM] * len(args), out_s...  180 us
    pallas_call x3, Pallas kernels, block_sums(): pl.pallas_call(functools.partial(blocks_kernel, first), out_shape=out_sha...  54.3 us
    unnamed x21, local copies, waits for them, and re-layouts  5.81 us

profile of v2, /device:TPU:1, one launch (start us, length us, event | category | flops | bytes accessed | tf_op | source)
XLA Modules:
  0.0 244.5 jit_solution(17124796538249815163)
XLA Ops:
  0.6 0.0 copy-start
  0.6 0.0 copy-start.4
  0.7 0.0 copy-start.5
  0.7 0.0 copy-start.6
  0.7 0.7 iota_compare_fusion
  1.4 1.0 copy.19
  2.5 0.1 fusion
  2.6 0.6 copy.17
  3.2 0.7 compare_select_fusion
  3.9 0.1 copy.15
  4.0 0.1 reshape.87
  4.1 0.9 gather_fusion
  5.0 0.1 copy.13
  5.1 0.1 reshape_squeeze.6.user_tile
  5.2 0.1 copy.14
  5.2 0.1 reshape_squeeze.7.word_tile
  5.3 0.0 copy-done.3
  5.3 31.0 %comm0.1 = bf16[2,4,4,8,32,128]{5,4,3,2,1,0:T(8,128)(2,1)S(1)} custom-call(f32[32,128]{1,0:T(8,128)S(1)} %copy-done.3), custom_call_target="tpu_custom_call" | custom-call | tf_op jit(solution)/shard_map/comm0/pallas_call | solution.py:249
  36.3 0.0 copy-done.4
  36.4 0.0 copy-done.2
  36.4 0.0 copy-start.1
  36.4 3.4 %copy-done.1 = bf16[1,1,32,8,128,128]{5,4,3,2,1,0:T(8,128)(2,1)S(1)} copy-done((bf16[1,1,32,8,128,128]{5,4,3,2,1,0:T(8,128)(2,1)S(1)}, bf16[1,1,32,8,128,128]{5,4,3,2,1,0:T(8,128)(2,1)}, u32[]{:S(2)}) %copy-start.1) | copy-done | bytes 8388632
  39.7 21.4 %blocks_first.1 = (f32[256,32,128]{2,1,0:T(8,128)S(1)}, bf16[32,8,128,128]{3,2,1,0:T(8,128)(2,1)S(1)}) custom-call(s32[256]{0:T(256)S(1)} %reshape_squeeze.6.user_tile, s32[256]{0:T(256)S(1)} %reshape_squeeze.7.word_tile, s32[32]{0:T(128)S(1)} %bitcast.37, bf16[256,32,128]{2,1,0:T(8,128)(2,1)S(1)} %bitcast.29, bf16[8,128,128]{2,1,0:T(8,128)(2,1)S(1)} %bitcast.31, ...), custom_call_target="tpu_custom_call" | custom-call | tf_op jit(solution)/shard_map/blocks_first/pallas_call | solution.py:390
  61.2 0.0 copy-done.7
  61.2 0.1 broadcast_in_dim.23.activity
  61.3 49.9 %comm1.1 = (f32[32,128]{1,0:T(8,128)S(1)}, f32[8,128]{1,0:T(8,128)S(1)}, bf16[2,4,4,8,32,128]{5,4,3,2,1,0:T(8,128)(2,1)S(1)}) custom-call(f32[2,4,4,8,32,128]{5,4,3,2,1,0:T(8,128)S(1)} %bitcast.30, f32[32,128]{1,0:T(8,128)S(1)} %copy-done.3, f32[32,128]{1,0:T(8,128)S(1)} %broadcast_in_dim.23.activity), custom_call_target="tpu_custom_call" | custom-call | tf_op jit(solution)/shard_map/comm1/pallas_call | solution.py:249
  111.2 16.4 %blocks_next.2 = f32[256,32,128]{2,1,0:T(8,128)S(1)} custom-call(s32[256]{0:T(256)S(1)} %reshape_squeeze.6.user_tile, s32[256]{0:T(256)S(1)} %reshape_squeeze.7.word_tile, s32[32]{0:T(128)S(1)} %bitcast.38, bf16[256,32,128]{2,1,0:T(8,128)(2,1)S(1)} %bitcast.35, bf16[8,128,128]{2,1,0:T(8,128)(2,1)S(1)} %bitcast.32, ...), custom_call_target="tpu_custom_call" | custom-call | tf_op jit(solution)/shard_map/blocks_next/pallas_call | solution.py:390
  127.6 59.0 %comm2.1 = (f32[32,128]{1,0:T(8,128)S(1)}, f32[32,128]{1,0:T(8,128)S(1)}, f32[32,128]{1,0:T(8,128)S(1)}, f32[8,128]{1,0:T(8,128)S(1)}, bf16[2,4,4,8,32,128]{5,4,3,2,1,0:T(8,128)(2,1)S(1)}) custom-call(f32[2,4,4,8,32,128]{5,4,3,2,1,0:T(8,128)S(1)} %bitcast.26, f32[32,128]{1,0:T(8,128)S(1)} %copy-done.3, f32[32,128]{1,0:T(8,128)S(1)} %broadcast_in_dim.23.activity, ...), custom_call_target="tpu_custom_call" | custom-call | tf_op jit(solution)/shard_map/comm2/pallas_call | solution.py:249
  186.6 16.4 %blocks_next.3 = f32[256,32,128]{2,1,0:T(8,128)S(1)} custom-call(s32[256]{0:T(256)S(1)} %reshape_squeeze.6.user_tile, s32[256]{0:T(256)S(1)} %reshape_squeeze.7.word_tile, s32[32]{0:T(128)S(1)} %bitcast.39, bf16[256,32,128]{2,1,0:T(8,128)(2,1)S(1)} %bitcast.34, bf16[8,128,128]{2,1,0:T(8,128)(2,1)S(1)} %bitcast.33, ...), custom_call_target="tpu_custom_call" | custom-call | tf_op jit(solution)/shard_map/blocks_next/pallas_call | solution.py:390
  203.0 40.2 %comm3.1 = (f32[32,128]{1,0:T(8,128)S(1)}, f32[32,128]{1,0:T(8,128)S(1)}) custom-call(f32[2,4,4,8,32,128]{5,4,3,2,1,0:T(8,128)S(1)} %bitcast.25, f32[32,128]{1,0:T(8,128)S(1)} %broadcast_in_dim.23.activity, f32[32,128]{1,0:T(8,128)S(1)} %get-tuple-element.15.residual.before, f32[32,128]{1,0:T(8,128)S(1)} %get-tuple-element.18.residual, ...), custom_call_target="tpu_custom_call" | custom-call | tf_op jit(solution)/shard_map/comm3/pallas_call | solution.py:249
  243.3 0.6 copy.22
  243.9 0.6 copy.23
  (9 shorter events, 0.1 us)
Async XLA Ops:
  0.6 3.5 %copy-start = (bf16[2048,128]{1,0:T(8,128)(2,1)S(1)}, bf16[2048,128]{1,0:T(8,128)(2,1)}, u32[]{:S(2)}) copy-start(bf16[2048,128]{1,0:T(8,128)(2,1)} %param.13) | copy-start | bytes 1572868
  0.6 35.7 %copy-start.4 = (s32[1,1,32]{2,1,0:T(1,128)S(1)}, s32[1,1,32]{2,1,0:T(1,128)}, u32[]{:S(2)}) copy-start(s32[1,1,32]{2,1,0:T(1,128)} %param.18) | copy-start | bytes 388
  0.7 4.3 %copy-start.5 = (s32[1,1,32,8]{2,3,1,0:T(8,128)S(1)}, s32[1,1,32,8]{2,3,1,0:T(8,128)}, u32[]{:S(2)}) copy-start(s32[1,1,32,8]{2,3,1,0:T(8,128)} %param.15) | copy-start | bytes 3076
  0.7 4.5 %copy-start.6 = (s32[1,1,32,8]{2,3,1,0:T(8,128)S(1)}, s32[1,1,32,8]{2,3,1,0:T(8,128)}, u32[]{:S(2)}) copy-start(s32[1,1,32,8]{2,3,1,0:T(8,128)} %param.16) | copy-start | bytes 3076
  0.7 35.7 %copy-start.2 = (bf16[1,8,128,128]{3,2,1,0:T(8,128)(2,1)S(1)}, bf16[1,8,128,128]{3,2,1,0:T(8,128)(2,1)}, u32[]{:S(2)}) copy-start(bf16[1,8,128,128]{3,2,1,0:T(8,128)(2,1)} %param.12) | copy-start | bytes 786436
  0.7 4.7 %copy-start.3 = (f32[32,128]{1,0:T(8,128)S(1)}, f32[32,128]{1,0:T(8,128)}, u32[]{:S(2)}) copy-start(f32[32,128]{1,0:T(8,128)} %start.5) | copy-start | bytes 49156
  36.4 3.4 %copy-start.1 = (bf16[1,1,32,8,128,128]{5,4,3,2,1,0:T(8,128)(2,1)S(1)}, bf16[1,1,32,8,128,128]{5,4,3,2,1,0:T(8,128)(2,1)}, u32[]{:S(2)}) copy-start(bf16[1,1,32,8,128,128]{5,4,3,2,1,0:T(8,128)(2,1)} %param.14) | copy-start | bytes 25165828
  39.7 21.4 %copy-start.7 = (f32[32]{0:T(128)S(1)}, f32[32]{0:T(128)}, u32[]{:S(2)}) copy-start(f32[32]{0:T(128)} %param.11) | copy-start | bytes 388

commit v3 on v2

--- a/solution.py
+++ b/solution.py
@@ -66,56 +66,78 @@
     pl.semaphore_wait(barrier, len(partners))
 
 
-def reduce_scatter(here, part, core_in, p_out, p_in, q_out, q_in, z_out, z_in, c_sem, p_sem, q_sem, z_sem):
+def reduce_scatter(here, part, scratch):
+    core_in, p_out, relay, p_in, q_out, q_in, z_out, z_in, c_sem, p_sem, q_sem, z_sem = scratch
     c, p, q, z = here
+    other = device(1 - c, q, p, z)
+    up, down = device(c, (p + 1) % NP, q, z), device(c, (p + 3) % NP, q, z)
     copies = []
     core = {}
-    for k in (1, 2, 3, 0):
+    for k in (2, 1, 3, 0):
         pp = (q + k) % NP
-        core[k] = send(part.at[1 - c, pp], core_in.at[pp], c_sem, k, device(1 - c, q, p, z))
+        core[k] = send(part.at[1 - c, pp], core_in.at[pp], c_sem, k, other)
         copies.append(core[k])
+
+    def fill(slot, k, h, relayed):
+        pp = (p + k) % NP
+
+        def body(i, carry):
+            value = part[c, pp, 2 * h + i] + core_in[pp, 2 * h + i]
+            if relayed:
+                value = value + relay[h, i].astype(F32)
+            p_out[slot, i] = value.astype(BF16)
+            return carry
+
+        lax.fori_loop(0, 2, body, 0)
+
+    core[2].wait_recv()
+    fill(0, 2, 0, False)
+    far = [send(p_out.at[0], relay.at[0], p_sem, 0, up)]
+    fill(1, 2, 1, False)
+    far.append(send(p_out.at[1], relay.at[1], p_sem, 1, down))
+    core[1].wait_recv()
+    fill(2, 1, 1, False)
+    near = [send(p_out.at[2], p_in.at[0, 1], p_sem, 2, up)]
+    core[3].wait_recv()
+    fill(3, 3, 0, False)
+    near.append(send(p_out.at[3], p_in.at[1, 0], p_sem, 3, down))
+    far[0].wait_recv()
+    fill(4, 1, 0, True)
+    near.append(send(p_out.at[4], p_in.at[0, 0], p_sem, 4, up))
+    far[1].wait_recv()
+    fill(5, 3, 1, True)
+    near.append(send(p_out.at[5], p_in.at[1, 1], p_sem, 5, down))
+    copies += far + near
+    core[0].wait_recv()
+    for copy in near:
+        copy.wait_recv()
+
+    def chunk(qq):
+        h, i = qq // 2, qq % 2
+        total = part[c, p, qq] + core_in[p, qq]
+        return total + p_in[0, h, i].astype(F32) + p_in[1, h, i].astype(F32)
+
     ring = {}
-    for k in range(1, NP):
-        pp = (p + k) % NP
-        core[k].wait_recv()
-
-        def to_send(i, carry):
-            p_out[k - 1, i] = (part[c, pp, i] + core_in[pp, i]).astype(BF16)
-            return carry
-
-        lax.fori_loop(0, NQ, to_send, 0)
-        ring[k] = send(p_out.at[k - 1], p_in.at[k - 1], p_sem, k, device(c, pp, q, z))
-        copies.append(ring[k])
-    core[0].wait_recv()
-    for k in range(1, NP):
-        ring[k].wait_recv()
-
-    def chunk(qq):
-        total = part[c, p, qq] + core_in[p, qq]
-        for k in range(1, NP):
-            total = total + p_in[k - 1, qq].astype(F32)
-        return total
-
-    ring = {}
-    for k in range(1, NQ):
+    for k in (2, 1, 3):
         qq = (q + k) % NQ
         q_out[k - 1] = chunk(qq).astype(BF16)
         ring[k] = send(q_out.at[k - 1], q_in.at[k - 1], q_sem, k, device(c, p, qq, z))
         copies.append(ring[k])
     total = chunk(q)
-    for k in range(1, NQ):
+    for k in (1, 3, 2):
         ring[k].wait_recv()
         total = total + q_in[k - 1].astype(F32)
-    z_out[...] = total
+    z_out[...] = total.astype(BF16)
     ring = {}
-    for k in range(1, NZ):
+    order = (4, 3, 5, 2, 6, 1, 7)
+    for k in order:
         zz = (z + k) % NZ
         ring[k] = send(z_out.at[zz], z_in.at[k - 1], z_sem, k, device(c, p, q, zz))
         copies.append(ring[k])
-    rows = z_out[z]
-    for k in range(1, NZ):
+    rows = z_out[z].astype(F32)
+    for k in order[::-1]:
         ring[k].wait_recv()
-        rows = rows + z_in[k - 1]
+        rows = rows + z_in[k - 1].astype(F32)
     for copy in copies:
         copy.wait_send()
     return rows
@@ -164,40 +186,69 @@
 
 def gather(here, rows, out, sems, total=None, tile=None):
     c, p, q, z = here
-    c_sem, p_sem, q_sem, z_sem = sems
-    copies = []
-
-    def note(stage, value):
-        if total is not None:
-            total.start(stage, value)
+    c_sem, p_sem, h_sem, q_sem, z_sem = sems
+    other = device(1 - c, q, p, z)
+    up, down = device(c, (p + 1) % NP, q, z), device(c, (p + 3) % NP, q, z)
+    half = NZ // 2
+    copies, core = [], []
 
     out[c, p, q, z] = rows.astype(BF16)
     mine = out.at[c, p, q, z]
-    ring = [send(mine, mine, z_sem, k, device(c, p, q, (z + k) % NZ)) for k in range(1, NZ)]
-    note("z", tile)
-    for copy in ring:
+    order = (4, 3, 5, 2, 6, 1, 7)
+    ring = [send(mine, mine, z_sem, k, device(c, p, q, (z + k) % NZ)) for k in order]
+    if total is not None:
+        total.start("z", tile)
+    for copy in ring[::-1]:
         copy.wait_recv()
     copies += ring
+
+    def across(ref):
+        core.append(send(ref, ref, c_sem, len(core), other))
+
+    direct = []
+
+    def along(j, qq):
+        ref = out.at[c, p, qq]
+        direct.append((send(ref, ref, p_sem, 2 * j, up), send(ref, ref, p_sem, 2 * j + 1, down)))
+        copies.extend(direct[-1])
+
+    halves = []
+
+    def onward(j, qq):
+        direct[j][0].wait_recv()
+        ref = out.at[c, (p + 3) % NP, qq, pl.ds(0, half)]
+        first = send(ref, ref, h_sem, 2 * j, up)
+        direct[j][1].wait_recv()
+        ref = out.at[c, (p + 1) % NP, qq, pl.ds(half, half)]
+        second = send(ref, ref, h_sem, 2 * j + 1, down)
+        halves.append((first, second))
+        copies.extend(halves[-1])
+        across(out.at[c, (p + 3) % NP, qq])
+        across(out.at[c, (p + 1) % NP, qq])
+
+    steps = (0, 1, 3, 2)
     mine = out.at[c, p, q]
-    ring = [send(mine, mine, q_sem, k, device(c, p, (q + k) % NQ, z)) for k in range(1, NQ)]
+    ring = {k: send(mine, mine, q_sem, k, device(c, p, (q + k) % NQ, z)) for k in (2, 1, 3)}
+    copies += ring.values()
+    along(0, q)
+    across(mine)
     if total is not None:
-        note("q", total.finish())
-    for copy in ring:
-        copy.wait_recv()
-    copies += ring
-    mine = out.at[c, p]
-    ring = [send(mine, mine, p_sem, k, device(c, (p + k) % NP, q, z)) for k in range(1, NP)]
-    copies += ring
-    other = device(1 - c, q, p, z)
-    core = [send(mine, mine, c_sem, 0, other)]
+        total.start("q", total.finish())
+    for j in range(1, NQ):
+        qq = (q - steps[j] + NQ) % NQ
+        ring[steps[j]].wait_recv()
+        along(j, qq)
+        across(out.at[c, p, qq])
+        onward(j - 1, (q - steps[j - 1] + NQ) % NQ)
     if total is not None:
-        note("p", total.finish())
-    for k, copy in enumerate(ring, 1):
-        copy.wait_recv()
-        arrived = out.at[c, (p - k + NP) % NP]
-        core.append(send(arrived, arrived, c_sem, k, other))
+        total.start("p", total.finish())
+    onward(NQ - 1, (q - steps[-1] + NQ) % NQ)
+    for j in range(NQ):
+        for copy in halves[j]:
+            copy.wait_recv()
+        across(out.at[c, (p + 2) % NP, (q - steps[j] + NQ) % NQ])
     if total is not None:
-        note("c", total.finish())
+        total.start("c", total.finish())
         tile = total.finish()
         total.close()
     for copy in core:
@@ -220,20 +271,22 @@
 
 SCATTER_SCRATCH = [
     pltpu.VMEM((NP, NQ, NZ, ROWS, R), F32),
-    pltpu.VMEM((NP - 1, NQ, NZ, ROWS, R), BF16),
-    pltpu.VMEM((NP - 1, NQ, NZ, ROWS, R), BF16),
+    pltpu.VMEM((6, 2, NZ, ROWS, R), BF16),
+    pltpu.VMEM((2, 2, NZ, ROWS, R), BF16),
+    pltpu.VMEM((2, 2, 2, NZ, ROWS, R), BF16),
     pltpu.VMEM((NQ - 1, NZ, ROWS, R), BF16),
     pltpu.VMEM((NQ - 1, NZ, ROWS, R), BF16),
-    pltpu.VMEM((NZ, ROWS, R), F32),
-    pltpu.VMEM((NZ - 1, ROWS, R), F32),
+    pltpu.VMEM((NZ, ROWS, R), BF16),
+    pltpu.VMEM((NZ - 1, ROWS, R), BF16),
     pltpu.SemaphoreType.DMA((2, NP)),
-    pltpu.SemaphoreType.DMA((2, NP)),
+    pltpu.SemaphoreType.DMA((2, 6)),
     pltpu.SemaphoreType.DMA((2, NQ)),
     pltpu.SemaphoreType.DMA((2, NZ)),
 ]
 GATHER_SCRATCH = [
-    pltpu.SemaphoreType.DMA((2, NP)),
-    pltpu.SemaphoreType.DMA((2, NP)),
+    pltpu.SemaphoreType.DMA((2, NP * NQ)),
+    pltpu.SemaphoreType.DMA((2, 2 * NQ)),
+    pltpu.SemaphoreType.DMA((2, 2 * NQ)),
     pltpu.SemaphoreType.DMA((2, NQ)),
     pltpu.SemaphoreType.DMA((2, NZ)),
 ]
@@ -268,7 +321,7 @@
 def residual_kernel(part, start, activity, residual, square, out, *scratch):
     here = place()
     enter(here)
-    rows = reduce_scatter(here, part, *scratch[:N_S])
+    rows = reduce_scatter(here, part, scratch[:N_S])
     r = activity[...] * rows - RIDGE * start[...]
     residual[...] = r
     total = Sum(here, scratch[N_S + N_G :])
@@ -278,7 +331,7 @@
 def step_kernel(part, start, activity, residual, square, solution, later, image, new, out, *scratch):
     here = place()
     enter(here)
-    rows = reduce_scatter(here, part, *scratch[:N_S])
+    rows = reduce_scatter(here, part, scratch[:N_S])
     r = residual[...]
     q = activity[...] * rows + RIDGE * r
     image[...] = q
@@ -295,7 +348,7 @@
 def last_kernel(part, activity, before, residual, square, image, new, solution, out, left, *scratch):
     here = place()
     enter(here)
-    rows = reduce_scatter(here, part, *scratch[:N_S])
+    rows = reduce_scatter(here, part, scratch[:N_S])
     r = residual[...]
     rr = all_of(new[...])
     ratio = rr / all_of(square[...])

time: 245 us -> 241 us (0.984)
  Pallas kernels: 234 us -> 230 us
    pallas_call x4, Pallas kernels: 180 us -> 176 us  [communicate(): pl.pallas_call(kernel, out_shape=outs, in_specs=[VMEM] * len(args), out_s...]
where the time goes in v3:
time: 241 us; the launch traced here: 240 us
  Pallas kernels  230 us (95%)
  local copies, waits for them, and re-layouts  7.71 us (3%)
    pallas_call x4, Pallas kernels, communicate(): pl.pallas_call(kernel, out_shape=outs, in_specs=[VMEM] * len(args), out_s...  176 us
    pallas_call x3, Pallas kernels, block_sums(): pl.pallas_call(functools.partial(blocks_kernel, first), out_shape=out_sha...  54.3 us
    unnamed x21, local copies, waits for them, and re-layouts  5.81 us

profile of v3, /device:TPU:1, one launch (start us, length us, event | category | flops | bytes accessed | tf_op | source)
XLA Modules:
  0.0 240.5 jit_solution(14975790894951000563)
XLA Ops:
  0.6 0.0 copy-start
  0.6 0.0 copy-start.4
  0.7 0.0 copy-start.5
  0.7 0.0 copy-start.6
  0.7 0.0 copy-start.2
  0.7 0.0 copy-start.3
  0.7 0.7 iota_compare_fusion
  1.4 1.0 copy.19
  2.5 0.1 fusion
  2.6 0.6 copy.17
  3.2 0.7 compare_select_fusion
  3.9 0.1 copy.15
  4.0 0.1 reshape.87
  4.1 0.0 copy-done
  4.1 0.9 gather_fusion
  5.0 0.1 copy.13
  5.1 0.1 reshape_squeeze.6.user_tile
  5.2 0.0 copy-done.6
  5.2 0.1 copy.14
  5.2 0.1 reshape_squeeze.7.word_tile
  5.3 32.0 %comm0.1 = bf16[2,4,4,8,32,128]{5,4,3,2,1,0:T(8,128)(2,1)S(1)} custom-call(f32[32,128]{1,0:T(8,128)S(1)} %copy-done.3), custom_call_target="tpu_custom_call" | custom-call | tf_op jit(solution)/shard_map/comm0/pallas_call | solution.py:302
  37.4 0.0 copy-start.1
  37.4 3.4 %copy-done.1 = bf16[1,1,32,8,128,128]{5,4,3,2,1,0:T(8,128)(2,1)S(1)} copy-done((bf16[1,1,32,8,128,128]{5,4,3,2,1,0:T(8,128)(2,1)S(1)}, bf16[1,1,32,8,128,128]{5,4,3,2,1,0:T(8,128)(2,1)}, u32[]{:S(2)}) %copy-start.1) | copy-done | bytes 8388632
  40.8 21.4 %blocks_first.1 = (f32[256,32,128]{2,1,0:T(8,128)S(1)}, bf16[32,8,128,128]{3,2,1,0:T(8,128)(2,1)S(1)}) custom-call(s32[256]{0:T(256)S(1)} %reshape_squeeze.6.user_tile, s32[256]{0:T(256)S(1)} %reshape_squeeze.7.word_tile, s32[32]{0:T(128)S(1)} %bitcast.37, bf16[256,32,128]{2,1,0:T(8,128)(2,1)S(1)} %bitcast.29, bf16[8,128,128]{2,1,0:T(8,128)(2,1)S(1)} %bitcast.31, ...), custom_call_target="tpu_custom_call" | custom-call | tf_op jit(solution)/shard_map/blocks_first/pallas_call | solution.py:443
  62.2 0.1 broadcast_in_dim.23.activity
  62.3 47.9 %comm1.1 = (f32[32,128]{1,0:T(8,128)S(1)}, f32[8,128]{1,0:T(8,128)S(1)}, bf16[2,4,4,8,32,128]{5,4,3,2,1,0:T(8,128)(2,1)S(1)}) custom-call(f32[2,4,4,8,32,128]{5,4,3,2,1,0:T(8,128)S(1)} %bitcast.30, f32[32,128]{1,0:T(8,128)S(1)} %copy-done.3, f32[32,128]{1,0:T(8,128)S(1)} %broadcast_in_dim.23.activity), custom_call_target="tpu_custom_call" | custom-call | tf_op jit(solution)/shard_map/comm1/pallas_call | solution.py:302
  110.2 16.4 %blocks_next.2 = f32[256,32,128]{2,1,0:T(8,128)S(1)} custom-call(s32[256]{0:T(256)S(1)} %reshape_squeeze.6.user_tile, s32[256]{0:T(256)S(1)} %reshape_squeeze.7.word_tile, s32[32]{0:T(128)S(1)} %bitcast.38, bf16[256,32,128]{2,1,0:T(8,128)(2,1)S(1)} %bitcast.35, bf16[8,128,128]{2,1,0:T(8,128)(2,1)S(1)} %bitcast.32, ...), custom_call_target="tpu_custom_call" | custom-call | tf_op jit(solution)/shard_map/blocks_next/pallas_call | solution.py:443
  126.7 58.4 %comm2.1 = (f32[32,128]{1,0:T(8,128)S(1)}, f32[32,128]{1,0:T(8,128)S(1)}, f32[32,128]{1,0:T(8,128)S(1)}, f32[8,128]{1,0:T(8,128)S(1)}, bf16[2,4,4,8,32,128]{5,4,3,2,1,0:T(8,128)(2,1)S(1)}) custom-call(f32[2,4,4,8,32,128]{5,4,3,2,1,0:T(8,128)S(1)} %bitcast.26, f32[32,128]{1,0:T(8,128)S(1)} %copy-done.3, f32[32,128]{1,0:T(8,128)S(1)} %broadcast_in_dim.23.activity, ...), custom_call_target="tpu_custom_call" | custom-call | tf_op jit(solution)/shard_map/comm2/pallas_call | solution.py:302
  185.0 16.4 %blocks_next.3 = f32[256,32,128]{2,1,0:T(8,128)S(1)} custom-call(s32[256]{0:T(256)S(1)} %reshape_squeeze.6.user_tile, s32[256]{0:T(256)S(1)} %reshape_squeeze.7.word_tile, s32[32]{0:T(128)S(1)} %bitcast.39, bf16[256,32,128]{2,1,0:T(8,128)(2,1)S(1)} %bitcast.34, bf16[8,128,128]{2,1,0:T(8,128)(2,1)S(1)} %bitcast.33, ...), custom_call_target="tpu_custom_call" | custom-call | tf_op jit(solution)/shard_map/blocks_next/pallas_call | solution.py:443
  201.5 37.7 %comm3.1 = (f32[32,128]{1,0:T(8,128)S(1)}, f32[32,128]{1,0:T(8,128)S(1)}) custom-call(f32[2,4,4,8,32,128]{5,4,3,2,1,0:T(8,128)S(1)} %bitcast.25, f32[32,128]{1,0:T(8,128)S(1)} %broadcast_in_dim.23.activity, f32[32,128]{1,0:T(8,128)S(1)} %get-tuple-element.15.residual.before, f32[32,128]{1,0:T(8,128)S(1)} %get-tuple-element.18.residual, ...), custom_call_target="tpu_custom_call" | custom-call | tf_op jit(solution)/shard_map/comm3/pallas_call | solution.py:302
  239.2 0.6 copy.22
  239.8 0.6 copy.23
  (9 shorter events, 0.1 us)
Async XLA Ops:
  0.6 3.5 %copy-start = (bf16[2048,128]{1,0:T(8,128)(2,1)S(1)}, bf16[2048,128]{1,0:T(8,128)(2,1)}, u32[]{:S(2)}) copy-start(bf16[2048,128]{1,0:T(8,128)(2,1)} %param.13) | copy-start | bytes 1572868
  0.6 36.7 %copy-start.4 = (s32[1,1,32]{2,1,0:T(1,128)S(1)}, s32[1,1,32]{2,1,0:T(1,128)}, u32[]{:S(2)}) copy-start(s32[1,1,32]{2,1,0:T(1,128)} %param.18) | copy-start | bytes 388
  0.7 4.3 %copy-start.5 = (s32[1,1,32,8]{2,3,1,0:T(8,128)S(1)}, s32[1,1,32,8]{2,3,1,0:T(8,128)}, u32[]{:S(2)}) copy-start(s32[1,1,32,8]{2,3,1,0:T(8,128)} %param.15) | copy-start | bytes 3076
  0.7 4.5 %copy-start.6 = (s32[1,1,32,8]{2,3,1,0:T(8,128)S(1)}, s32[1,1,32,8]{2,3,1,0:T(8,128)}, u32[]{:S(2)}) copy-start(s32[1,1,32,8]{2,3,1,0:T(8,128)} %param.16) | copy-start | bytes 3076
  0.7 36.7 %copy-start.2 = (bf16[1,8,128,128]{3,2,1,0:T(8,128)(2,1)S(1)}, bf16[1,8,128,128]{3,2,1,0:T(8,128)(2,1)}, u32[]{:S(2)}) copy-start(bf16[1,8,128,128]{3,2,1,0:T(8,128)(2,1)} %param.12) | copy-start | bytes 786436
  0.7 4.7 %copy-start.3 = (f32[32,128]{1,0:T(8,128)S(1)}, f32[32,128]{1,0:T(8,128)}, u32[]{:S(2)}) copy-start(f32[32,128]{1,0:T(8,128)} %start.5) | copy-start | bytes 49156
  37.4 3.4 %copy-start.1 = (bf16[1,1,32,8,128,128]{5,4,3,2,1,0:T(8,128)(2,1)S(1)}, bf16[1,1,32,8,128,128]{5,4,3,2,1,0:T(8,128)(2,1)}, u32[]{:S(2)}) copy-start(bf16[1,1,32,8,128,128]{5,4,3,2,1,0:T(8,128)(2,1)} %param.14) | copy-start | bytes 25165828
  40.8 21.4 %copy-start.7 = (f32[32]{0:T(128)S(1)}, f32[32]{0:T(128)}, u32[]{:S(2)}) copy-start(f32[32]{0:T(128)} %param.11) | copy-start | bytes 388

commit v4 on v1

v4 whole, which is shorter than its diff:
```python
import jax
import jax.numpy as jnp
from jax import lax
from jax.experimental import pallas as pl
from jax.experimental.pallas import tpu as pltpu
from jax.sharding import PartitionSpec as P

TILE = 128
R = 128
UT = 2
SLOTS = 8
GROUPS = 32
NP = 4
NQ = 4
NZ = 8
ROWS = 32
RIDGE = 0.05
MESH = pl.DeviceIdType.MESH
F32 = jnp.float32
BF16 = jnp.bfloat16
VMEM = pl.BlockSpec(memory_space=pltpu.VMEM)


def place():
    loop = lax.axis_index("loop")
    own = lax.axis_index("own")
    c = loop % 2
    x = (own // 4) * 2 + (loop // 2) % 2
    y = own % 4
    z = loop // 4
    return c, x * (1 - c) + y * c, y * (1 - c) + x * c, z


def device(c, p, q, z):
    x = p * (1 - c) + q * c
    y = q * (1 - c) + p * c
    return {"loop": (z * 2 + x % 2) * 2 + c, "own": (x // 2) * 4 + y}


def send(src, dst, sems, k, to):
    copy = pltpu.make_async_remote_copy(
        src_ref=src,
        dst_ref=dst,
        send_sem=sems.at[0, k],
        recv_sem=sems.at[1, k],
        device_id=to,
        device_id_type=MESH,
    )
    copy.start()
    return copy


def enter(here):
    c, p, q, z = here
    barrier = pltpu.get_barrier_semaphore()
    partners = [device(1 - c, q, p, z)]
    partners += [device(c, (p + k) % NP, q, z) for k in range(1, NP)]
    partners += [device(c, p, (q + k) % NQ, z) for k in range(1, NQ)]
    partners += [device(c, p, q, (z + k) % NZ) for k in range(1, NZ)]
    for partner in partners:
        pl.semaphore_signal(barrier, inc=1, device_id=partner, device_id_type=MESH)
    pl.semaphore_wait(barrier, len(partners))


def to_partner(here, part, core_in, c_sem):
    c, p, q, z = here
    core = {}
    for k in (2, 1, 3, 0):
        pp = (q + k) % NP
        core[k] = send(part.at[1 - c, pp], core_in.at[pp], c_sem, k, device(1 - c, q, p, z))
    return core


def reduce_scatter(here, part, core, scratch):
    core_in, p_out, relay, p_in, q_out, q_in, z_out, z_in, p_sem, q_sem, z_sem = scratch
    c, p, q, z = here
    up, down = device(c, (p + 1) % NP, q, z), device(c, (p + 3) % NP, q, z)
    copies = list(core.values())

    def fill(slot, k, h, relayed):
        pp = (p + k) % NP

        def body(i, carry):
            value = part[c, pp, 2 * h + i] + core_in[pp, 2 * h + i]
            if relayed:
                value = value + relay[h, i].astype(F32)
            p_out[slot, i] = value.astype(BF16)
            return carry

        lax.fori_loop(0, 2, body, 0)

    core[2].wait_recv()
    fill(0, 2, 0, False)
    far = [send(p_out.at[0], relay.at[0], p_sem, 0, up)]
    fill(1, 2, 1, False)
    far.append(send(p_out.at[1], relay.at[1], p_sem, 1, down))
    core[1].wait_recv()
    fill(2, 1, 1, False)
    near = [send(p_out.at[2], p_in.at[0, 1], p_sem, 2, up)]
    core[3].wait_recv()
    fill(3, 3, 0, False)
    near.append(send(p_out.at[3], p_in.at[1, 0], p_sem, 3, down))
    far[0].wait_recv()
    fill(4, 1, 0, True)
    near.append(send(p_out.at[4], p_in.at[0, 0], p_sem, 4, up))
    far[1].wait_recv()
    fill(5, 3, 1, True)
    near.append(send(p_out.at[5], p_in.at[1, 1], p_sem, 5, down))
    copies += far + near
    core[0].wait_recv()
    for copy in near:
        copy.wait_recv()

    def chunk(qq):
        h, i = qq // 2, qq % 2
        total = part[c, p, qq] + core_in[p, qq]
        return total + p_in[0, h, i].astype(F32) + p_in[1, h, i].astype(F32)

    ring = {}
    for k in (2, 1, 3):
        qq = (q + k) % NQ
        q_out[k - 1] = chunk(qq).astype(BF16)
        ring[k] = send(q_out.at[k - 1], q_in.at[k - 1], q_sem, k, device(c, p, qq, z))
        copies.append(ring[k])
    total = chunk(q)
    for k in (1, 3, 2):
        ring[k].wait_recv()
        total = total + q_in[k - 1].astype(F32)
    z_out[...] = total.astype(BF16)
    ring = {}
    order = (4, 3, 5, 2, 6, 1, 7)
    for k in order:
        zz = (z + k) % NZ
        ring[k] = send(z_out.at[zz], z_in.at[k - 1], z_sem, k, device(c, p, q, zz))
        copies.append(ring[k])
    rows = z_out[z].astype(F32)
    for k in order[::-1]:
        ring[k].wait_recv()
        rows = rows + z_in[k - 1].astype(F32)
    for copy in copies:
        copy.wait_send()
    return rows


class Sum:
    def __init__(self, here, refs):
        self.here = here
        self.slots, self.sems = refs
        self.copies = []

    def start(self, stage, tile):
        c, p, q, z = self.here
        slots, sems = self.slots, self.sems
        place_in, to, base = {
            "z": (z, [device(c, p, q, (z + k) % NZ) for k in range(1, NZ)], 0),
            "q": (q, [device(c, p, (q + k) % NQ, z) for k in range(1, NQ)], 8),
            "p": (p, [device(c, (p + k) % NP, q, z) for k in range(1, NP)], 12),
            "c": (c, [device(1 - c, q, p, z)], 16),
        }[stage]
        self.base, self.size = base, len(to) + 1
        mine = slots.at[base + place_in]
        mine[...] = tile
        self.now = [send(mine, mine, sems, base + k, d) for k, d in enumerate(to)]
        self.copies += self.now

    def finish(self):
        for copy in self.now:
            copy.wait_recv()
        total = self.slots[self.base]
        for k in range(1, self.size):
            total = total + self.slots[self.base + k]
        return total

    def close(self):
        for copy in self.copies:
            copy.wait_send()

    def whole(self, tile):
        for stage in ("z", "q", "p", "c"):
            self.start(stage, tile)
            tile = self.finish()
        self.close()
        return tile


def gather(here, rows, out, sems, total=None, tile=None, meanwhile=None):
    c, p, q, z = here
    c_sem, p_sem, q_sem, z_sem = sems
    copies = []

    def note(stage, value):
        if total is not None:
            total.start(stage, value)

    out[c, p, q, z] = rows.astype(BF16)
    mine = out.at[c, p, q, z]
    ring = [send(mine, mine, z_sem, k, device(c, p, q, (z + k) % NZ)) for k in (4, 3, 5, 2, 6, 1, 7)]
    note("z", tile)
    if meanwhile is not None:
        meanwhile(0)
    for copy in ring:
        copy.wait_recv()
    copies += ring
    mine = out.at[c, p, q]
    ring = [send(mine, mine, q_sem, k, device(c, p, (q + k) % NQ, z)) for k in range(1, NQ)]
    if total is not None:
        note("q", total.finish())
    if meanwhile is not None:
        meanwhile(1)
    for copy in ring:
        copy.wait_recv()
    copies += ring
    mine = out.at[c, p]
    ring = [send(mine, mine, p_sem, k, device(c, (p + k) % NP, q, z)) for k in range(1, NP)]
    copies += ring
    other = device(1 - c, q, p, z)
    core = [send(mine, mine, c_sem, 0, other)]
    if total is not None:
        note("p", total.finish())
    if meanwhile is not None:
        meanwhile(2)
    for k, copy in enumerate(ring, 1):
        copy.wait_recv()
        arrived = out.at[c, (p - k + NP) % NP]
        core.append(send(arrived, arrived, c_sem, k, other))
    if total is not None:
        note("c", total.finish())
        tile = total.finish()
        total.close()
    for copy in core:
        copy.wait_recv()
    for copy in copies + core:
        copy.wait_send()
    return tile


def folded(values):
    tile = values[0:8]
    for k in range(1, ROWS // 8):
        tile = tile + values[8 * k : 8 * k + 8]
    return tile


def all_of(tile):
    return jnp.sum(tile, keepdims=True)


def masks(run, mask, begin, end):
    columns = lax.broadcasted_iota(jnp.int32, (TILE, TILE), 1)

    def group(g, carry):
        here = run[g]
        for s in range(SLOTS):
            first, length = here[:, 2 * s : 2 * s + 1], here[:, 2 * s + 1 : 2 * s + 2]
            seen = ((columns - first) & (TILE - 1)) < length
            mask[g, s] = jnp.where(seen, 1.0, 0.0).astype(BF16)
        return carry

    lax.fori_loop(begin, end, group, 0)


def block_sums(core, whole, words, subs, user_tile, word_tile, mask, ratings, part):
    def group(n, carry):
        g = 2 * n + core
        xl, z = n % 2, n // 2

        def rows_at(ref, u, y):
            x = 2 * u + xl
            return ref.at[core, x * (1 - core) + y * core, y * (1 - core) + x * core, z]

        sub_rows = subs[g]
        work = []
        for s in range(SLOTS):
            u = user_tile[g * SLOTS + s]
            rows = jnp.concatenate([rows_at(whole, u, y)[...] for y in range(4)], axis=0)
            word = words[word_tile[g * SLOTS + s]].astype(F32)
            products = (word * sub_rows[s : s + 1]).astype(BF16)
            scores = lax.dot_general(rows, products, (((1,), (1,)), ((), ())), preferred_element_type=F32)
            work.append((s, u, products, scores))
        top, low = [], []
        for s, u, products, scores in work:
            if ratings is not None:
                scores = ratings[g, s].astype(F32) - scores
            weights = scores.astype(BF16) * mask[g, s]
            lower = weights * jnp.full((TILE, TILE), u, jnp.int32).astype(F32).astype(BF16)
            top.append(weights - lower)
            low.append(lower)
        both = jnp.concatenate([jnp.concatenate(top, 1), jnp.concatenate(low, 1)], 0)
        products = jnp.concatenate([w[2] for w in work], 0)
        sums = jnp.dot(both, products, preferred_element_type=F32)
        for u in range(UT):
            for y in range(4):
                at = u * TILE + ROWS * y
                rows_at(part, u, y)[...] = sums[at : at + ROWS]
        return carry

    lax.fori_loop(0, GROUPS // 2, group, 0)


DMA = pltpu.SemaphoreType.DMA
SCATTER_SCRATCH = [
    pltpu.VMEM((NP, NQ, NZ, ROWS, R), F32),
    pltpu.VMEM((6, 2, NZ, ROWS, R), BF16),
    pltpu.VMEM((2, 2, NZ, ROWS, R), BF16),
    pltpu.VMEM((2, 2, 2, NZ, ROWS, R), BF16),
    pltpu.VMEM((NQ - 1, NZ, ROWS, R), BF16),
    pltpu.VMEM((NQ - 1, NZ, ROWS, R), BF16),
    pltpu.VMEM((NZ, ROWS, R), BF16),
    pltpu.VMEM((NZ - 1, ROWS, R), BF16),
    DMA((2, 6)),
    DMA((2, NQ)),
    DMA((2, NZ)),
]
GATHER_SCRATCH = [DMA((2, NP)), DMA((2, NP)), DMA((2, NQ)), DMA((2, NZ))]
SUM_SCRATCH = [pltpu.VMEM((18, 8, R), F32), DMA((2, 17))]
WHOLE = pltpu.VMEM((2, NP, NQ, NZ, ROWS, R), BF16)
BLOCKS = pltpu.VMEM((GROUPS, SLOTS, TILE, TILE), BF16)
SCRATCH = [WHOLE] * 3 + [pltpu.VMEM((2, NP, NQ, NZ, ROWS, R), F32), BLOCKS, BLOCKS, DMA, DMA((2, NP))]
N_S, N_G, N_SUM, N_OWN = len(SCATTER_SCRATCH), len(GATHER_SCRATCH), len(SUM_SCRATCH), len(SCRATCH)


def step_kernel(start, activity, words, subs, run, user_tile, word_tile, ratings, out, left, *scratch):
    whole0, whole1, whole2, part, mask, held, fetch_sem, core_sem = scratch[:N_OWN]
    scatter = scratch[N_OWN : N_OWN + N_S]
    at = N_OWN + N_S
    gather_sems = scratch[at : at + N_G]
    sums = [scratch[at + N_G + i * N_SUM : at + N_G + (i + 1) * N_SUM] for i in range(4)]
    here = place()
    fetch = pltpu.make_async_copy(ratings, held, fetch_sem)
    fetch.start()
    enter(here)

    def data(whole, values):
        c = here[0]
        block_sums(1 - c, whole, words, subs, user_tile, word_tile, mask, values, part)
        core = to_partner(here, part, scatter[0], core_sem)
        block_sums(c, whole, words, subs, user_tile, word_tile, mask, values, part)
        return activity[...] * reduce_scatter(here, part, core, scatter)

    cuts = (0, 11, 22, GROUPS)
    gather(here, start[...], whole0, gather_sems, meanwhile=lambda i: masks(run, mask, cuts[i], cuts[i + 1]))
    fetch.wait()
    r = data(whole0, held) - RIDGE * start[...]
    rr = all_of(gather(here, r, whole1, gather_sems, Sum(here, sums[0]), folded(r * r)))
    q = data(whole1, None) + RIDGE * r
    step = rr / all_of(Sum(here, sums[1]).whole(folded(r * q)))
    solution = start[...] + step * r
    later = r - step * q
    new = all_of(gather(here, later, whole2, gather_sems, Sum(here, sums[2]), folded(later * later)))
    ratio = new / rr
    d = later + ratio * r
    q = data(whole2, None) + RIDGE * later + ratio * q
    step = new / all_of(Sum(here, sums[3]).whole(folded(d * q)))
    out[...] = solution + step * d
    left[...] = later - step * q


def on_device(
    factor_start,
    activity,
    word_factors,
    sub_factors,
    ratings,
    user_tile,
    word_tile,
    subreddit,
    counts,
    runs,
):
    live = counts[0, 0]
    subs = sub_factors[subreddit[0, 0]].astype(F32)
    used = jnp.arange(SLOTS)[None, :] < live[:, None]
    lengths = jnp.where(used[:, :, None], runs[0, 0][:, :, 1, :], 0)
    run = jnp.stack([runs[0, 0][:, :, 0, :], lengths], axis=2)
    run = run.reshape(GROUPS, 2 * SLOTS, TILE).transpose(0, 2, 1)
    scale = jnp.broadcast_to(activity[:, None], (ROWS, R))
    table = pl.BlockSpec(memory_space=pltpu.SMEM)
    block = jax.ShapeDtypeStruct((ROWS, R), F32)
    return tuple(
        pl.pallas_call(
            step_kernel,
            out_shape=[block, block],
            in_specs=[VMEM] * 5 + [table] * 2 + [pl.BlockSpec(memory_space=pl.ANY)],
            out_specs=[VMEM] * 2,
            scratch_shapes=SCRATCH + SCATTER_SCRATCH + GATHER_SCRATCH + SUM_SCRATCH * 4,
            compiler_params=pltpu.CompilerParams(
                collective_id=0, has_side_effects=True, vmem_limit_bytes=56 << 20
            ),
            name="step",
        )(
            factor_start,
            scale,
            word_factors[0],
            subs,
            run,
            user_tile[0, 0].reshape(-1),
            word_tile[0, 0].reshape(-1),
            ratings[0, 0],
        )
    )


def solution(mesh):
    placed = (
        P(("loop", "own"), None),
        P(("loop", "own")),
        P("loop", None, None, None),
        P(),
        P("loop", "own", None, None, None, None),
        P("loop", "own", None, None),
        P("loop", "own", None, None),
        P("loop", "own", None, None),
        P("loop", "own", None),
        P("loop", "own", None, None, None, None),
    )
    return jax.shard_map(
        on_device,
        mesh=mesh,
        in_specs=placed,
        out_specs=(P(("loop", "own"), None), P(("loop", "own"), None)),
        check_vma=False,
    )
```

time: 332 us -> 218 us (0.66)
  Pallas kernels: 323 us -> 204 us
    pallas_call x7 -> x1, Pallas kernels: 323 us -> 204 us  [on_device(): pl.pallas_call(step_kernel, out_shape=[block, block], in_specs=[VMEM] * 5...]
where the time goes in v4:
time: 218 us
  Pallas kernels  204 us (94%)
  local copies, waits for them, and re-layouts  10.9 us (5%)
    pallas_call x1, Pallas kernels, on_device(): pl.pallas_call(step_kernel, out_shape=[block, block], in_specs=[VMEM] * 5...  204 us
    unnamed x7, local copies, waits for them, and re-layouts  5.27 us

profile of v4, /device:TPU:1, one launch (start us, length us, event | category | flops | bytes accessed | tf_op | source)
XLA Modules:
  0.0 218.0 jit_solution(3542088467801375825)
XLA Ops:
  0.6 0.0 copy-start
  0.6 1.1 copy.19
  1.7 0.7 iota_compare_fusion
  2.4 0.1 fusion
  2.5 2.0 copy.15
  4.5 0.7 compare_select_fusion
  5.2 0.1 copy.13
  5.3 0.1 reshape.63
  5.4 0.0 copy-done
  5.4 0.9 gather_fusion
  6.2 0.7 bitcast_convert_fusion.subs
  6.9 0.8 copy.16
  7.7 0.7 reshape_squeeze.6.user_tile
  8.3 0.8 copy.17
  9.1 0.7 reshape_squeeze.7.word_tile
  9.8 1.3 broadcast_in_dim.14.activity
  11.1 204.3 %step.1 = (f32[32,128]{1,0:T(8,128)}, f32[32,128]{1,0:T(8,128)}) custom-call(f32[32,128]{1,0:T(8,128)} %start.1, f32[32,128]{1,0:T(8,128)} %broadcast_in_dim.14.activity, bf16[8,128,128]{2,1,0:T(8,128)(2,1)} %bitcast.23, f32[32,8,128]{2,1,0:T(8,128)} %bitcast_convert_fusion.subs, s32[32,128,16]{2,1,0:T(8,128)} %bitcast.20, s32[256]{0:T(256)} %reshape_squeeze.6.user_tile, ...), custom_call_target="tpu_custom_call" | custom-call | tf_op jit(solution)/shard_map/step/pallas_call | solution.py:380
  215.4 1.3 copy.22
  216.7 1.3 copy.23
  (2 shorter events, 0.0 us)
Async XLA Ops:
  0.6 4.7 %copy-start = (bf16[2048,128]{1,0:T(8,128)(2,1)S(1)}, bf16[2048,128]{1,0:T(8,128)(2,1)}, u32[]{:S(2)}) copy-start(bf16[2048,128]{1,0:T(8,128)(2,1)} %param.13) | copy-start | bytes 1572868

commit v5 on v4

v5 whole, which is shorter than its diff:
```python
import jax
import jax.numpy as jnp
from jax import lax
from jax.experimental import pallas as pl
from jax.experimental.pallas import tpu as pltpu
from jax.sharding import PartitionSpec as P

TILE = 128
R = 128
UT = 2
SLOTS = 8
SUBS = 2048
GROUPS = 32
NP = 4
NQ = 4
NZ = 8
ROWS = 32
RIDGE = 0.05
MESH = pl.DeviceIdType.MESH
F32 = jnp.float32
BF16 = jnp.bfloat16
VMEM = pl.BlockSpec(memory_space=pltpu.VMEM)


def place():
    loop = lax.axis_index("loop")
    own = lax.axis_index("own")
    c = loop % 2
    x = (own // 4) * 2 + (loop // 2) % 2
    y = own % 4
    z = loop // 4
    return c, x * (1 - c) + y * c, y * (1 - c) + x * c, z


def device(c, p, q, z):
    x = p * (1 - c) + q * c
    y = q * (1 - c) + p * c
    return {"loop": (z * 2 + x % 2) * 2 + c, "own": (x // 2) * 4 + y}


def send(src, dst, sems, k, to):
    copy = pltpu.make_async_remote_copy(
        src_ref=src,
        dst_ref=dst,
        send_sem=sems.at[0, k],
        recv_sem=sems.at[1, k],
        device_id=to,
        device_id_type=MESH,
    )
    copy.start()
    return copy


def enter(here):
    c, p, q, z = here
    barrier = pltpu.get_barrier_semaphore()
    partners = [device(1 - c, q, (p + k) % NQ, z) for k in range(NQ)]
    partners += [device(1 - c, (q + k) % NP, p, z) for k in range(1, NP)]
    partners += [device(c, (p + k) % NP, q, z) for k in range(1, NP)]
    partners += [device(c, p, (q + k) % NQ, z) for k in range(1, NQ)]
    partners += [device(c, p, q, (z + k) % NZ) for k in range(1, NZ)]
    for partner in partners:
        pl.semaphore_signal(barrier, inc=1, device_id=partner, device_id_type=MESH)
    pl.semaphore_wait(barrier, len(partners))


def to_partner(here, part, core_in, c_sem):
    c, p, q, z = here
    core = {}
    for k in (2, 1, 3, 0):
        pp = (q + k) % NP
        core[k] = send(part.at[1 - c, pp], core_in.at[pp], c_sem, k, device(1 - c, q, p, z))
    return core


def reduce_scatter(here, part, core, scratch, total=None, weigh=None, own=None):
    core_in, p_out, relay, p_in, q_out, q_in, z_out, z_in, p_sem, q_sem, z_sem = scratch
    c, p, q, z = here
    up, down = device(c, (p + 1) % NP, q, z), device(c, (p + 3) % NP, q, z)
    copies = list(core.values())

    def fill(slot, k, h, relayed):
        pp = (p + k) % NP

        def body(i, carry):
            value = part[c, pp, 2 * h + i] + core_in[pp, 2 * h + i]
            if relayed:
                value = value + relay[h, i].astype(F32)
            p_out[slot, i] = value.astype(BF16)
            return carry

        lax.fori_loop(0, 2, body, 0)

    core[2].wait_recv()
    fill(0, 2, 0, False)
    far = [send(p_out.at[0], relay.at[0], p_sem, 0, up)]
    fill(1, 2, 1, False)
    far.append(send(p_out.at[1], relay.at[1], p_sem, 1, down))
    core[1].wait_recv()
    fill(2, 1, 1, False)
    near = [send(p_out.at[2], p_in.at[0, 1], p_sem, 2, up)]
    core[3].wait_recv()
    fill(3, 3, 0, False)
    near.append(send(p_out.at[3], p_in.at[1, 0], p_sem, 3, down))
    far[0].wait_recv()
    fill(4, 1, 0, True)
    near.append(send(p_out.at[4], p_in.at[0, 0], p_sem, 4, up))
    far[1].wait_recv()
    fill(5, 3, 1, True)
    near.append(send(p_out.at[5], p_in.at[1, 1], p_sem, 5, down))
    copies += far + near
    core[0].wait_recv()
    for copy in near:
        copy.wait_recv()

    def chunk(qq):
        h, i = qq // 2, qq % 2
        total = part[c, p, qq] + core_in[p, qq]
        return total + p_in[0, h, i].astype(F32) + p_in[1, h, i].astype(F32)

    ring = {}
    dots = own
    for k in (2, 1, 3):
        qq = (q + k) % NQ
        value = chunk(qq)
        q_out[k - 1] = value.astype(BF16)
        if total is not None:
            dots = dots + eighths(weigh(qq) * value)
        ring[k] = send(q_out.at[k - 1], q_in.at[k - 1], q_sem, k, device(c, p, qq, z))
        copies.append(ring[k])
    value = chunk(q)
    if total is not None:
        total.start("q", dots + eighths(weigh(q) * value))
    for k in (1, 3, 2):
        ring[k].wait_recv()
        value = value + q_in[k - 1].astype(F32)
    z_out[...] = value.astype(BF16)
    ring = {}
    order = (4, 3, 5, 2, 6, 1, 7)
    for k in order:
        zz = (z + k) % NZ
        ring[k] = send(z_out.at[zz], z_in.at[k - 1], z_sem, k, device(c, p, q, zz))
        copies.append(ring[k])
    if total is not None:
        total.start("z", total.finish())
    rows = z_out[z].astype(F32)
    for k in order[::-1]:
        ring[k].wait_recv()
        rows = rows + z_in[k - 1].astype(F32)
    if total is not None:
        total.start("rest", total.finish())
    for copy in copies:
        copy.wait_send()
    return rows


class Sum:
    def __init__(self, here, refs):
        self.here = here
        self.slots, self.sems = refs
        self.copies = []

    def start(self, stage, tile):
        c, p, q, z = self.here
        slots, sems = self.slots, self.sems
        at, others = {
            "z": (z, [device(c, p, q, (z + k) % NZ) for k in range(1, NZ)]),
            "q": (8 + q, [device(c, p, (q + k) % NQ, z) for k in range(1, NQ)]),
            "rest": (12 + p, [device(c, (p + k) % NP, q, z) for k in range(1, NP)]),
        }[stage]
        first = {"z": 0, "q": 8, "rest": 12}[stage]
        self.used = (first, first + (8 if stage != "q" else 4))
        mine = slots.at[at]
        mine[...] = tile
        self.now = [send(mine, mine, sems, first + k, d) for k, d in enumerate(others)]
        if stage == "rest":
            across = slots.at[16 + p]
            self.now += [send(mine, across, sems, 16 + k, device(1 - c, q, (p + k) % NQ, z)) for k in range(NQ)]
        self.copies += self.now

    def finish(self):
        for copy in self.now:
            copy.wait_recv()
        begin, end = self.used
        total = self.slots[begin]
        for k in range(begin + 1, min(end, begin + 4)):
            total = total + self.slots[k]
        if end > begin + 4:
            rest = self.slots[begin + 4]
            for k in range(begin + 5, end):
                rest = rest + self.slots[k]
            total = total + rest
        return total

    def close(self):
        tile = self.finish()
        for copy in self.copies:
            copy.wait_send()
        return all_of(tile)


def gather(here, rows, out, sems, total=None, tile=None, scales=None, scale_sems=None, meanwhile=None):
    c, p, q, z = here
    c_sem, p_sem, q_sem, z_sem = sems
    other = device(1 - c, q, p, z)
    copies, core = [], []

    def pause(i):
        if meanwhile is not None:
            meanwhile(i)

    def across(ref):
        core.append(send(ref, ref, c_sem, len(core), other))

    out[c, p, q, z] = rows.astype(BF16)
    mine = out.at[c, p, q, z]
    order = (4, 3, 5, 2, 6, 1, 7)
    ring = [send(mine, mine, z_sem, k, device(c, p, q, (z + k) % NZ)) for k in order]
    if scales is not None:
        mine = scales.at[q, z]
        ring += [send(mine, mine, scale_sems, k, device(c, p, q, (z + k) % NZ)) for k in order]
    if total is not None:
        total.start("z", tile)
    pause(0)
    for copy in ring:
        copy.wait_recv()
    copies += ring

    pieces = {}

    def along(j, qq):
        ref = out.at[c, p, qq]
        for k in (2, 1, 3):
            pieces[j, k] = send(ref, ref, p_sem, 4 * j + k, device(c, (p + k) % NP, q, z))
        across(ref)

    mine = out.at[c, p, q]
    ring = {k: send(mine, mine, q_sem, k, device(c, p, (q + k) % NQ, z)) for k in (2, 1, 3)}
    copies += ring.values()
    if scales is not None:
        mine = scales.at[q]
        beside = [send(mine, mine, scale_sems, 8 + k, device(c, p, (q + k) % NQ, z)) for k in (2, 1, 3)]
        copies += beside
    along(0, q)
    if total is not None:
        total.start("q", total.finish())
    pause(1)
    steps = (0, 1, 3, 2)
    for j in range(1, NQ):
        ring[steps[j]].wait_recv()
        along(j, (q - steps[j] + NQ) % NQ)
    if total is not None:
        total.start("rest", total.finish())
    pause(2)
    if scales is not None:
        for copy in beside:
            copy.wait_recv()
    for j in range(NQ):
        for k in (1, 3, 2):
            pieces[j, k].wait_recv()
            across(out.at[c, (p - k + NP) % NP, (q - steps[j] + NQ) % NQ])
    for copy in core:
        copy.wait_recv()
    for copy in copies + core + list(pieces.values()):
        copy.wait_send()


def folded(values):
    tile = values[0:8]
    for k in range(1, ROWS // 8):
        tile = tile + values[8 * k : 8 * k + 8]
    return tile


def eighths(values):
    tile = folded(values[0])
    for k in range(1, NZ):
        tile = tile + folded(values[k])
    return tile


def all_of(tile):
    return jnp.sum(tile, keepdims=True)


def masks(runs, counts, mask, begin, end):
    columns = lax.broadcasted_iota(jnp.int32, (TILE, TILE), 1)

    def group(g, carry):
        both = jnp.concatenate([runs[g, s] for s in range(SLOTS)], axis=0).T
        live = counts[g]
        for s in range(SLOTS):
            length = jnp.where(s < live, both[:, 2 * s + 1 : 2 * s + 2], 0)
            seen = ((columns - both[:, 2 * s : 2 * s + 1]) & (TILE - 1)) < length
            mask[g, s] = jnp.where(seen, 1.0, 0.0).astype(BF16)
        return carry

    lax.fori_loop(begin, end, group, 0)


def widen(narrow, wide):
    def body(i, carry):
        at = pl.multiple_of(i * TILE, TILE)
        wide[pl.ds(at, TILE)] = narrow[pl.ds(at, TILE)].astype(F32)
        return carry

    lax.fori_loop(0, SUBS // TILE, body, 0)


def columns_of(scales, wide):
    rows = lax.broadcasted_iota(jnp.int32, (ROWS, R), 0)
    lanes = lax.broadcasted_iota(jnp.int32, (ROWS, R), 1)

    def body(i, carry):
        for z in range(NZ):
            picked = jnp.where(rows == lanes, scales[i, z, 0:1], 0.0)
            wide[i, z] = jnp.broadcast_to(jnp.sum(picked, axis=1, keepdims=True), (ROWS, R))
        return carry

    lax.fori_loop(0, NQ, body, 0)


def block_sums(core, whole, words, subs, tables, mask, ratings, part):
    user_tile, word_tile, subreddit = tables

    def group(n, carry):
        g = 2 * n + core
        xl, z = n % 2, n // 2

        def rows_at(ref, u, y):
            x = 2 * u + xl
            return ref.at[core, x * (1 - core) + y * core, y * (1 - core) + x * core, z]

        work = []
        for s in range(SLOTS):
            u = user_tile[s, g]
            rows = jnp.concatenate([rows_at(whole, u, y)[...] for y in range(4)], axis=0)
            products = words[word_tile[s, g]] * subs[pl.ds(subreddit[s, g], 1)].astype(BF16)
            scores = lax.dot_general(rows, products, (((1,), (1,)), ((), ())), preferred_element_type=F32)
            work.append((s, u, products, scores))
        top, low = [], []
        for s, u, products, scores in work:
            if ratings is not None:
                scores = ratings[g, s].astype(F32) - scores
            weights = scores.astype(BF16) * mask[g, s]
            lower = weights * jnp.full((TILE, TILE), u, jnp.int32).astype(F32).astype(BF16)
            top.append(weights - lower)
            low.append(lower)
        both = jnp.concatenate([jnp.concatenate(top, 1), jnp.concatenate(low, 1)], 0)
        products = jnp.concatenate([w[2] for w in work], 0)
        sums = jnp.dot(both, products, preferred_element_type=F32)
        for u in range(UT):
            for y in range(4):
                at = u * TILE + ROWS * y
                rows_at(part, u, y)[...] = sums[at : at + ROWS]
        return carry

    lax.fori_loop(0, GROUPS // 2, group, 0)


DMA = pltpu.SemaphoreType.DMA
SCATTER_SCRATCH = [
    pltpu.VMEM((NP, NQ, NZ, ROWS, R), F32),
    pltpu.VMEM((6, 2, NZ, ROWS, R), BF16),
    pltpu.VMEM((2, 2, NZ, ROWS, R), BF16),
    pltpu.VMEM((2, 2, 2, NZ, ROWS, R), BF16),
    pltpu.VMEM((NQ - 1, NZ, ROWS, R), BF16),
    pltpu.VMEM((NQ - 1, NZ, ROWS, R), BF16),
    pltpu.VMEM((NZ, ROWS, R), BF16),
    pltpu.VMEM((NZ - 1, ROWS, R), BF16),
    DMA((2, 6)),
    DMA((2, NQ)),
    DMA((2, NZ)),
]
GATHER_SCRATCH = [DMA((2, NP * NQ)), DMA((2, NP * NQ)), DMA((2, NQ)), DMA((2, NZ))]
SUM_SCRATCH = [pltpu.VMEM((20, 8, R), F32), DMA((2, 20))]
WHOLE = pltpu.VMEM((2, NP, NQ, NZ, ROWS, R), BF16)
BLOCKS = pltpu.VMEM((GROUPS, SLOTS, TILE, TILE), BF16)
SCRATCH = [WHOLE] * 3 + [
    pltpu.VMEM((2, NP, NQ, NZ, ROWS, R), F32),
    BLOCKS,
    BLOCKS,
    DMA,
    DMA((2, NP)),
    pltpu.VMEM((SUBS, R), F32),
    pltpu.VMEM((NQ, NZ, 8, R), F32),
    pltpu.VMEM((NQ, NZ, ROWS, R), F32),
    DMA((2, 12)),
]
N_S, N_G, N_SUM, N_OWN = len(SCATTER_SCRATCH), len(GATHER_SCRATCH), len(SUM_SCRATCH), len(SCRATCH)


def step_kernel(start, activity, words, subs, runs, counts, user_tile, word_tile, subreddit, ratings, out, left, *scratch):
    whole0, whole1, whole2, part, mask, held, fetch_sem, core_sem, wide, scales, scale, scale_sems = scratch[:N_OWN]
    scatter = scratch[N_OWN : N_OWN + N_S]
    at = N_OWN + N_S
    gather_sems = scratch[at : at + N_G]
    sums = [scratch[at + N_G + i * N_SUM : at + N_G + (i + 1) * N_SUM] for i in range(4)]
    tables = (user_tile, word_tile, subreddit)
    here = place()
    c, p, q, z = here
    fetch = pltpu.make_async_copy(ratings, held, fetch_sem)
    fetch.start()
    padded = jnp.concatenate([activity[...], jnp.zeros((1, R - ROWS), F32)], axis=1)
    scales[q, z] = jnp.broadcast_to(padded, (8, R))
    enter(here)

    def blocks(whole, values):
        block_sums(1 - c, whole, words, wide, tables, mask, values, part)
        core = to_partner(here, part, scatter[0], core_sem)
        block_sums(c, whole, words, wide, tables, mask, values, part)
        return core

    cuts = (0, 11, 22, GROUPS)

    def meanwhile(i):
        if i == 0:
            widen(subs, wide)
        masks(runs, counts, mask, cuts[i], cuts[i + 1])

    gather(here, start[...], whole0, gather_sems, scales=scales, scale_sems=scale_sems, meanwhile=meanwhile)
    columns_of(scales, scale)
    fetch.wait()
    core = blocks(whole0, held)
    scaled = scale[q, z]
    r = scaled * reduce_scatter(here, part, core, scatter) - RIDGE * start[...]
    norm = Sum(here, sums[0])
    gather(here, r, whole1, gather_sems, norm, folded(r * r))

    core = blocks(whole1, None)
    rr = norm.close()
    along = Sum(here, sums[1])
    rows = reduce_scatter(
        here, part, core, scatter, along, lambda qq: scale[qq] * whole1[c, p, qq].astype(F32), RIDGE * folded(r * r)
    )
    image = scaled * rows + RIDGE * r
    step = rr / along.close()
    solution = start[...] + step * r
    later = r - step * image
    norm = Sum(here, sums[2])
    gather(here, later, whole2, gather_sems, norm, folded(later * later))

    core = blocks(whole2, None)
    new = norm.close()
    ratio = new / rr
    d = later + ratio * r

    def weigh(qq):
        return scale[qq] * (whole2[c, p, qq].astype(F32) + ratio[:, :, None] * whole1[c, p, qq].astype(F32))

    along = Sum(here, sums[3])
    rest = RIDGE * later + ratio * image
    rows = reduce_scatter(here, part, core, scatter, along, weigh, folded(d * rest))
    step = new / along.close()
    out[...] = solution + step * d
    left[...] = later - step * (scaled * rows + rest)


def on_device(
    factor_start,
    activity,
    word_factors,
    sub_factors,
    ratings,
    user_tile,
    word_tile,
    subreddit,
    counts,
    runs,
):
    table = pl.BlockSpec(memory_space=pltpu.SMEM)
    block = jax.ShapeDtypeStruct((ROWS, R), F32)
    return tuple(
        pl.pallas_call(
            step_kernel,
            out_shape=[block, block],
            in_specs=[VMEM] * 5 + [table] * 4 + [pl.BlockSpec(memory_space=pl.ANY)],
            out_specs=[VMEM] * 2,
            scratch_shapes=SCRATCH + SCATTER_SCRATCH + GATHER_SCRATCH + SUM_SCRATCH * 4,
            compiler_params=pltpu.CompilerParams(
                collective_id=0, has_side_effects=True, vmem_limit_bytes=50 << 20
            ),
            name="step",
        )(
            factor_start,
            activity.reshape(1, ROWS),
            word_factors[0],
            sub_factors,
            runs[0, 0],
            counts[0, 0],
            user_tile[0, 0].T,
            word_tile[0, 0].T,
            subreddit[0, 0].T,
            ratings[0, 0],
        )
    )


def solution(mesh):
    placed = (
        P(("loop", "own"), None),
        P(("loop", "own")),
        P("loop", None, None, None),
        P(),
        P("loop", "own", None, None, None, None),
        P("loop", "own", None, None),
        P("loop", "own", None, None),
        P("loop", "own", None, None),
        P("loop", "own", None),
        P("loop", "own", None, None, None, None),
    )
    return jax.shard_map(
        on_device,
        mesh=mesh,
        in_specs=placed,
        out_specs=(P(("loop", "own"), None), P(("loop", "own"), None)),
        check_vma=False,
    )
```

time: 218 us -> 189 us (0.87)
  Pallas kernels: 204 us -> 180 us
  local copies, waits for them, and re-layouts: 10.9 us -> 8.23 us
    pallas_call x1, Pallas kernels: 204 us -> 180 us  [on_device(): pl.pallas_call(step_kernel, out_shape=[block, block], in_specs=[VMEM] * 5...]
    unnamed x7 -> x20, local copies, waits for them, and re-layouts: 5.27 us -> 8.23 us
where the time goes in v5:
time: 189 us
  Pallas kernels  180 us (95%)
  local copies, waits for them, and re-layouts  8.23 us (4%)
    pallas_call x1, Pallas kernels, on_device(): pl.pallas_call(step_kernel, out_shape=[block, block], in_specs=[VMEM] * 5...  180 us
    unnamed x20, local copies, waits for them, and re-layouts  8.23 us

profile of v5, /device:TPU:1, one launch (start us, length us, event | category | flops | bytes accessed | tf_op | source)
XLA Modules:
  0.0 188.8 jit_solution(16206658399772326983)
XLA Ops:
  0.6 0.0 copy-start
  0.6 1.0 copy-done
  1.7 0.0 copy-start.1
  1.7 0.9 copy-done.1
  2.6 0.0 copy-start.2
  2.6 0.9 copy-done.2
  3.6 0.0 copy-start.3
  3.6 0.7 copy-done.3
  4.3 0.0 copy-start.4
  4.3 0.7 copy-done.4
  5.0 0.0 copy-start.5
  5.0 0.7 copy-done.5
  5.7 0.0 copy-start.6
  5.7 0.7 copy-done.6
  6.4 0.0 copy-start.7
  6.4 0.7 copy-done.7
  7.0 0.0 copy-start.8
  7.0 0.7 copy-done.8
  7.7 179.9 %step.1 = (f32[32,128]{1,0:T(8,128)S(1)}, f32[32,128]{1,0:T(8,128)S(1)}) custom-call(f32[32,128]{1,0:T(8,128)S(1)} %copy-done.3, f32[1,32]{1,0:T(1,128)S(1)} %bitcast.19, bf16[8,128,128]{2,1,0:T(8,128)(2,1)S(1)} %bitcast.14, bf16[2048,128]{1,0:T(8,128)(2,1)S(1)} %copy-done, s32[32,8,2,128]{3,2,1,0:T(2,128)S(1)} %bitcast.15, s32[32]{0:T(128)S(1)} %bitcast.20, ...), custom_call_target="tpu_custom_call" | custom-call | tf_op jit(solution)/shard_map/step/pallas_call | solution.py:474
  187.6 0.6 copy.14
  188.2 0.6 copy.15
Async XLA Ops:
  0.6 1.0 copy-start
  1.7 0.9 copy-start.1
  2.6 0.9 copy-start.2
  3.6 0.7 copy-start.3
  4.3 0.7 copy-start.4
  5.0 0.7 copy-start.5
  5.7 0.7 copy-start.6
  6.4 0.7 copy-start.7
  7.0 0.7 copy-start.8

commit v6 on v5

--- a/solution.py
+++ b/solution.py
@@ -331,13 +331,21 @@
             x = 2 * u + xl
             return ref.at[core, x * (1 - core) + y * core, y * (1 - core) + x * core, z]
 
+        zero = jnp.zeros((TILE, R), BF16)
         work = []
-        for s in range(SLOTS):
-            u = user_tile[s, g]
-            rows = jnp.concatenate([rows_at(whole, u, y)[...] for y in range(4)], axis=0)
-            products = words[word_tile[s, g]] * subs[pl.ds(subreddit[s, g], 1)].astype(BF16)
-            scores = lax.dot_general(rows, products, (((1,), (1,)), ((), ())), preferred_element_type=F32)
-            work.append((s, u, products, scores))
+        for s in range(0, SLOTS, 2):
+            pair = []
+            for t in (s, s + 1):
+                u = user_tile[t, g]
+                rows = jnp.concatenate([rows_at(whole, u, y)[...] for y in range(4)], axis=0)
+                products = words[word_tile[t, g]] * subs[pl.ds(subreddit[t, g], 1)].astype(BF16)
+                pair.append((u, rows, products))
+            (u0, v0, p0), (u1, v1, p1) = pair
+            both = jnp.concatenate([jnp.concatenate([p0, zero], 1), jnp.concatenate([zero, p1], 1)], 0)
+            scores = lax.dot_general(
+                jnp.concatenate([v0, v1], 1), both, (((1,), (1,)), ((), ())), preferred_element_type=F32
+            )
+            work += [(s, u0, p0, scores[:, :TILE]), (s + 1, u1, p1, scores[:, TILE:])]
         top, low = [], []
         for s, u, products, scores in work:
             if ratings is not None:
@@ -355,7 +363,7 @@
                 rows_at(part, u, y)[...] = sums[at : at + ROWS]
         return carry
 
-    lax.fori_loop(0, GROUPS // 2, group, 0)
+    lax.fori_loop(0, GROUPS // 2, group, 0, unroll=4)
 
 
 DMA = pltpu.SemaphoreType.DMA
@@ -376,11 +384,22 @@
 SUM_SCRATCH = [pltpu.VMEM((20, 8, R), F32), DMA((2, 20))]
 WHOLE = pltpu.VMEM((2, NP, NQ, NZ, ROWS, R), BF16)
 BLOCKS = pltpu.VMEM((GROUPS, SLOTS, TILE, TILE), BF16)
+INPUTS = [
+    pltpu.VMEM((ROWS, R), F32),
+    pltpu.VMEM((1, ROWS), F32),
+    pltpu.VMEM((8, TILE, R), BF16),
+    pltpu.VMEM((SUBS, R), BF16),
+    pltpu.VMEM((GROUPS, SLOTS, 2, TILE), jnp.int32),
+    pltpu.SMEM((GROUPS,), jnp.int32),
+    pltpu.SMEM((SLOTS, GROUPS), jnp.int32),
+    pltpu.SMEM((SLOTS, GROUPS), jnp.int32),
+    pltpu.SMEM((SLOTS, GROUPS), jnp.int32),
+    BLOCKS,
+    DMA((10,)),
+]
 SCRATCH = [WHOLE] * 3 + [
     pltpu.VMEM((2, NP, NQ, NZ, ROWS, R), F32),
     BLOCKS,
-    BLOCKS,
-    DMA,
     DMA((2, NP)),
     pltpu.VMEM((SUBS, R), F32),
     pltpu.VMEM((NQ, NZ, 8, R), F32),
@@ -390,8 +409,12 @@
 N_S, N_G, N_SUM, N_OWN = len(SCATTER_SCRATCH), len(GATHER_SCRATCH), len(SUM_SCRATCH), len(SCRATCH)
 
 
-def step_kernel(start, activity, words, subs, runs, counts, user_tile, word_tile, subreddit, ratings, out, left, *scratch):
-    whole0, whole1, whole2, part, mask, held, fetch_sem, core_sem, wide, scales, scale, scale_sems = scratch[:N_OWN]
+def step_kernel(*refs):
+    given, (out, left), scratch = refs[:10], refs[10:12], refs[12:]
+    inputs, scratch = scratch[:11], scratch[11:]
+    fetch_sems = inputs[-1]
+    start, activity, words, subs, runs, counts, user_tile, word_tile, subreddit, held = inputs[:10]
+    whole0, whole1, whole2, part, mask, core_sem, wide, scales, scale, scale_sems = scratch[:N_OWN]
     scatter = scratch[N_OWN : N_OWN + N_S]
     at = N_OWN + N_S
     gather_sems = scratch[at : at + N_G]
@@ -399,11 +422,16 @@
     tables = (user_tile, word_tile, subreddit)
     here = place()
     c, p, q, z = here
-    fetch = pltpu.make_async_copy(ratings, held, fetch_sem)
-    fetch.start()
+    fetches = [pltpu.make_async_copy(given[i], inputs[i], fetch_sems.at[i]) for i in range(10)]
+    for fetch in fetches:
+        fetch.start()
+    for fetch in fetches[:2]:
+        fetch.wait()
     padded = jnp.concatenate([activity[...], jnp.zeros((1, R - ROWS), F32)], axis=1)
     scales[q, z] = jnp.broadcast_to(padded, (8, R))
     enter(here)
+    for fetch in fetches[2:9]:
+        fetch.wait()
 
     def blocks(whole, values):
         block_sums(1 - c, whole, words, wide, tables, mask, values, part)
@@ -420,7 +448,7 @@
 
     gather(here, start[...], whole0, gather_sems, scales=scales, scale_sems=scale_sems, meanwhile=meanwhile)
     columns_of(scales, scale)
-    fetch.wait()
+    fetches[9].wait()
     core = blocks(whole0, held)
     scaled = scale[q, z]
     r = scaled * reduce_scatter(here, part, core, scatter) - RIDGE * start[...]
@@ -468,17 +496,16 @@
     counts,
     runs,
 ):
-    table = pl.BlockSpec(memory_space=pltpu.SMEM)
     block = jax.ShapeDtypeStruct((ROWS, R), F32)
     return tuple(
         pl.pallas_call(
             step_kernel,
             out_shape=[block, block],
-            in_specs=[VMEM] * 5 + [table] * 4 + [pl.BlockSpec(memory_space=pl.ANY)],
+            in_specs=[pl.BlockSpec(memory_space=pl.ANY)] * 10,
             out_specs=[VMEM] * 2,
-            scratch_shapes=SCRATCH + SCATTER_SCRATCH + GATHER_SCRATCH + SUM_SCRATCH * 4,
+            scratch_shapes=INPUTS + SCRATCH + SCATTER_SCRATCH + GATHER_SCRATCH + SUM_SCRATCH * 4,
             compiler_params=pltpu.CompilerParams(
-                collective_id=0, has_side_effects=True, vmem_limit_bytes=50 << 20
+                collective_id=0, has_side_effects=True, vmem_limit_bytes=60 * 1024 * 1024
             ),
             name="step",
         )(

time: 189 us -> 169 us (0.89)
  Pallas kernels: 180 us -> 166 us
  local copies, waits for them, and re-layouts: 8.23 us -> 2.65 us
    pallas_call x1, Pallas kernels: 180 us -> 166 us  [on_device(): pl.pallas_call(step_kernel, out_shape=[block, block], in_specs=[pl.BlockS...]
    unnamed x20 -> x2, local copies, waits for them, and re-layouts: 8.23 us -> 2.65 us
where the time goes in v6:
time: 169 us
  Pallas kernels  166 us (98%)
  local copies, waits for them, and re-layouts  2.65 us (2%)
    pallas_call x1, Pallas kernels, on_device(): pl.pallas_call(step_kernel, out_shape=[block, block], in_specs=[pl.BlockS...  166 us

profile of v6, /device:TPU:1, one launch (start us, length us, event | category | flops | bytes accessed | tf_op | source)
XLA Modules:
  0.0 169.1 jit_solution(4364996839283283182)
XLA Ops:
  0.6 165.8 %step.1 = (f32[32,128]{1,0:T(8,128)}, f32[32,128]{1,0:T(8,128)}) custom-call(f32[32,128]{1,0:T(8,128)} %refs_0_.1, f32[1,32]{1,0:T(1,128)} %bitcast.20, bf16[8,128,128]{2,1,0:T(8,128)(2,1)} %bitcast.15, bf16[2048,128]{1,0:T(8,128)(2,1)} %refs_3_.1, s32[32,8,2,128]{3,2,1,0:T(2,128)} %bitcast.16, s32[32]{0:T(128)} %bitcast.21, s32[8,32]{1,0:T(8,128)} %bitcast.17, ...), custom_call_target="tpu_custom_call" | custom-call | tf_op jit(solution)/shard_map/step/pallas_call | solution.py:501
  166.4 1.3 copy.14
  167.8 1.3 copy.15

commit v7 on v6

--- a/solution.py
+++ b/solution.py
@@ -14,6 +14,7 @@
 NP = 4
 NQ = 4
 NZ = 8
+HALF = NZ // 2
 ROWS = 32
 RIDGE = 0.05
 MESH = pl.DeviceIdType.MESH
@@ -64,54 +65,76 @@
     pl.semaphore_wait(barrier, len(partners))
 
 
-def to_partner(here, part, core_in, c_sem):
+def to_partner(here, part, core_in, c_sem, t):
     c, p, q, z = here
+    zs = pl.ds(HALF * t, HALF)
     core = {}
     for k in (2, 1, 3, 0):
         pp = (q + k) % NP
-        core[k] = send(part.at[1 - c, pp], core_in.at[pp], c_sem, k, device(1 - c, q, p, z))
+        core[k] = send(part.at[1 - c, pp, :, zs], core_in.at[pp, :, zs], c_sem, NP * t + k, device(1 - c, q, p, z))
     return core
 
 
-def reduce_scatter(here, part, core, scratch, total=None, weigh=None, own=None):
+class FirstRing:
+    def __init__(self, here, part, core, scratch, t):
+        self.here, self.part, self.core, self.t = here, part, core, t
+        self.core_in, self.p_out, self.relay, self.p_in = scratch[:4]
+        self.sems = scratch[8]
+        self.zs = pl.ds(HALF * t, HALF)
+
+    def fill(self, slot, k, h, relayed):
+        c, p, _, _ = self.here
+        pp = (p + k) % NP
+        zs = self.zs
+
+        def body(i, carry):
+            value = self.part[c, pp, 2 * h + i, zs] + self.core_in[pp, 2 * h + i, zs]
+            if relayed:
+                value = value + self.relay[h, i, zs].astype(F32)
+            self.p_out[slot, i, zs] = value.astype(BF16)
+            return carry
+
+        lax.fori_loop(0, 2, body, 0)
+
+    def go(self, slot, to, k):
+        c, p, q, z = self.here
+        source = self.p_out.at[slot, :, self.zs]
+        return send(source, to.at[:, self.zs], self.sems, 6 * self.t + slot, device(c, (p + k) % NP, q, z))
+
+    def start(self):
+        self.core[2].wait_recv()
+        self.fill(0, 2, 0, False)
+        self.far = [self.go(0, self.relay.at[0], 1)]
+        self.fill(1, 2, 1, False)
+        self.far.append(self.go(1, self.relay.at[1], 3))
+        self.core[1].wait_recv()
+        self.fill(2, 1, 1, False)
+        self.near = [self.go(2, self.p_in.at[0, 1], 1)]
+        self.core[3].wait_recv()
+        self.fill(3, 3, 0, False)
+        self.near.append(self.go(3, self.p_in.at[1, 0], 3))
+
+    def pass_on(self):
+        self.far[0].wait_recv()
+        self.fill(4, 1, 0, True)
+        self.near.append(self.go(4, self.p_in.at[0, 0], 1))
+        self.far[1].wait_recv()
+        self.fill(5, 3, 1, True)
+        self.near.append(self.go(5, self.p_in.at[1, 1], 3))
+
+    def finish(self):
+        self.core[0].wait_recv()
+        for copy in self.near:
+            copy.wait_recv()
+        return list(self.core.values()) + self.far + self.near
+
+
+def reduce_scatter(here, part, rings, scratch, total=None, weigh=None, own=None):
     core_in, p_out, relay, p_in, q_out, q_in, z_out, z_in, p_sem, q_sem, z_sem = scratch
     c, p, q, z = here
-    up, down = device(c, (p + 1) % NP, q, z), device(c, (p + 3) % NP, q, z)
-    copies = list(core.values())
-
-    def fill(slot, k, h, relayed):
-        pp = (p + k) % NP
-
-        def body(i, carry):
-            value = part[c, pp, 2 * h + i] + core_in[pp, 2 * h + i]
-            if relayed:
-                value = value + relay[h, i].astype(F32)
-            p_out[slot, i] = value.astype(BF16)
-            return carry
-
-        lax.fori_loop(0, 2, body, 0)
-
-    core[2].wait_recv()
-    fill(0, 2, 0, False)
-    far = [send(p_out.at[0], relay.at[0], p_sem, 0, up)]
-    fill(1, 2, 1, False)
-    far.append(send(p_out.at[1], relay.at[1], p_sem, 1, down))
-    core[1].wait_recv()
-    fill(2, 1, 1, False)
-    near = [send(p_out.at[2], p_in.at[0, 1], p_sem, 2, up)]
-    core[3].wait_recv()
-    fill(3, 3, 0, False)
-    near.append(send(p_out.at[3], p_in.at[1, 0], p_sem, 3, down))
-    far[0].wait_recv()
-    fill(4, 1, 0, True)
-    near.append(send(p_out.at[4], p_in.at[0, 0], p_sem, 4, up))
-    far[1].wait_recv()
-    fill(5, 3, 1, True)
-    near.append(send(p_out.at[5], p_in.at[1, 1], p_sem, 5, down))
-    copies += far + near
-    core[0].wait_recv()
-    for copy in near:
-        copy.wait_recv()
+    copies = []
+    for ring in rings:
+        copies += ring.finish()
 
     def chunk(qq):
         h, i = qq // 2, qq % 2
@@ -320,10 +343,11 @@
     lax.fori_loop(0, NQ, body, 0)
 
 
-def block_sums(core, whole, words, subs, tables, mask, ratings, part):
+def block_sums(core_of, begin, end, whole, words, subs, tables, mask, ratings, part):
     user_tile, word_tile, subreddit = tables
 
     def group(n, carry):
+        core = core_of(n)
         g = 2 * n + core
         xl, z = n % 2, n // 2
 
@@ -363,7 +387,7 @@
                 rows_at(part, u, y)[...] = sums[at : at + ROWS]
         return carry
 
-    lax.fori_loop(0, GROUPS // 2, group, 0, unroll=4)
+    lax.fori_loop(begin, end, group, 0, unroll=4)
 
 
 DMA = pltpu.SemaphoreType.DMA
@@ -376,7 +400,7 @@
     pltpu.VMEM((NQ - 1, NZ, ROWS, R), BF16),
     pltpu.VMEM((NZ, ROWS, R), BF16),
     pltpu.VMEM((NZ - 1, ROWS, R), BF16),
-    DMA((2, 6)),
+    DMA((2, 12)),
     DMA((2, NQ)),
     DMA((2, NZ)),
 ]
@@ -400,7 +424,7 @@
 SCRATCH = [WHOLE] * 3 + [
     pltpu.VMEM((2, NP, NQ, NZ, ROWS, R), F32),
     BLOCKS,
-    DMA((2, NP)),
+    DMA((2, 2 * NP)),
     pltpu.VMEM((SUBS, R), F32),
     pltpu.VMEM((NQ, NZ, 8, R), F32),
     pltpu.VMEM((NQ, NZ, ROWS, R), F32),
@@ -434,10 +458,20 @@
         fetch.wait()
 
     def blocks(whole, values):
-        block_sums(1 - c, whole, words, wide, tables, mask, values, part)
-        core = to_partner(here, part, scatter[0], core_sem)
-        block_sums(c, whole, words, wide, tables, mask, values, part)
-        return core
+        rest = (whole, words, wide, tables, mask, values, part)
+        middle, end = GROUPS // 4, GROUPS // 2
+        block_sums(lambda n: 1 - c, 0, middle, *rest)
+        core = to_partner(here, part, scatter[0], core_sem, 0)
+        first = FirstRing(here, part, core, scatter, 0)
+        block_sums(lambda n: c + (1 - 2 * c) * (n // middle), 0, end, *rest)
+        core = to_partner(here, part, scatter[0], core_sem, 1)
+        second = FirstRing(here, part, core, scatter, 1)
+        first.start()
+        block_sums(lambda n: c, middle, end, *rest)
+        first.pass_on()
+        second.start()
+        second.pass_on()
+        return first, second
 
     cuts = (0, 11, 22, GROUPS)
 

time: 169 us -> 171 us (1.012)
  no operation moved by 1% of the time
where the time goes in v7:
time: 171 us; the launch traced here: 170 us
  Pallas kernels  167 us (98%)
  local copies, waits for them, and re-layouts  2.65 us (2%)
    pallas_call x1, Pallas kernels, on_device(): pl.pallas_call(step_kernel, out_shape=[block, block], in_specs=[pl.BlockS...  167 us

profile of v7, /device:TPU:1, one launch (start us, length us, event | category | flops | bytes accessed | tf_op | source)
XLA Modules:
  0.0 170.1 jit_solution(1555993269629312145)
XLA Ops:
  0.6 166.8 %step.1 = (f32[32,128]{1,0:T(8,128)}, f32[32,128]{1,0:T(8,128)}) custom-call(f32[32,128]{1,0:T(8,128)} %refs_0_.1, f32[1,32]{1,0:T(1,128)} %bitcast.20, bf16[8,128,128]{2,1,0:T(8,128)(2,1)} %bitcast.15, bf16[2048,128]{1,0:T(8,128)(2,1)} %refs_3_.1, s32[32,8,2,128]{3,2,1,0:T(2,128)} %bitcast.16, s32[32]{0:T(128)} %bitcast.21, s32[8,32]{1,0:T(8,128)} %bitcast.17, ...), custom_call_target="tpu_custom_call" | custom-call | tf_op jit(solution)/shard_map/step/pallas_call | solution.py:535
  167.4 1.3 copy.14
  168.7 1.3 copy.15
